TPU v7x, 128 devices: a whole 4x4x4 slice. The times are simulated.
128 devices in a mesh: sec: 4 (over y), col: 32 (over z, x, core).
Axes of the slice: x: 4, y: 4, z: 4, core: 2. Of those that a mesh axis runs over, the one named last changes fastest.
Arguments:
- column_state: float32 [4, 163840, 128], P('sec', 'col'), may hold values from -6 to 6
- mixing: float32 [4, 163840, 128], P('sec', 'col'), may hold values from 0.05 to 20
- surface_mask: int32 [4, 256, 128], P('sec', 'col'), may hold values 0 or 1
- pairings: int32 [4, 1728, 3], P('sec', 'col'), may hold values from 0 to 1023, as said below
- pairing_count: int32 [4, 32], P('sec', 'col'), may hold values from 3 to 54, as said below
- remap_weights: float32 [4, 65536, 128], P('sec', 'col'), may hold values from -0.5 to 0.5
Outputs:
- new_state: float32 [4, 163840, 128], P('sec', 'col')
Inputs may be any that keep to these rules, and one draw needn't show every extreme that they name: `pairings`: entry e of device d's list is used when e < pairing_count of d; used entries come first. Column 0 is a block of d, column 2 a weight block of d (below 16), column 1 a global block of the other component (ocean blocks for atmosphere devices, atmosphere blocks for ocean devices) on a device whose col differs from d's by -1, 0 or 1 cyclically. At most 6 used entries of one device name blocks of any one device. `pairing_count`: atmosphere devices use at most 18 entries.
All inputs are finite; a program needn't handle non-finite values. No bound on the sum of `surface_mask` on one device may be relied on, other than what follows from the above.
Results may differ from a plain program's by a relative error of at most 0.0003.
Values sent between devices are 32-bit elements; how exact they have to be, the bound alone decides.
No kernel may reach another device: no remote copies, remote signals or barrier semaphores. Data moves between devices by JAX's collectives and lax.ppermute only.
A program may use at most 192 MiB of HBM per device.

v0:
```python
from functools import partial

import jax
import jax.numpy as jnp
from jax import lax
from jax.sharding import PartitionSpec as P

LEV_ATM = 128
LEV_OCN = 80
TRC_ATM = 5
TRC_OCN = 8
COUPLED = 4
CAP = 6
SUBSTEPS = 2


highest = lax.Precision.HIGHEST


def from_above(field, stride, fill):
    head = jnp.full((stride,) + field.shape[1:], fill, field.dtype)
    return jnp.concatenate([head, field[:-stride]], axis=0)


def from_below(field, stride, fill):
    tail = jnp.full((stride,) + field.shape[1:], fill, field.dtype)
    return jnp.concatenate([field[stride:], tail], axis=0)


def tridiagonal(right_side, coupling, interface):
    shifted = jnp.concatenate([jnp.zeros_like(coupling[:1]), coupling[:-1]], axis=0)
    diagonal = 1.0 + shifted + coupling
    deepest = right_side.shape[0] - 1
    lower_band = -shifted
    upper_band = jnp.concatenate([-coupling[:-1], jnp.zeros_like(coupling[:1])], axis=0)
    source = right_side.at[deepest].add(coupling[deepest] * interface)
    stride = 1
    while stride <= deepest:
        diag_above = from_above(diagonal, stride, 1.0)
        diag_below = from_below(diagonal, stride, 1.0)
        factor_above = -lower_band / diag_above
        factor_below = -upper_band / diag_below
        new_diagonal = (
            diagonal
            + factor_above * from_above(upper_band, stride, 0.0)
            + factor_below * from_below(lower_band, stride, 0.0)
        )
        new_source = (
            source
            + factor_above * from_above(source, stride, 0.0)
            + factor_below * from_below(source, stride, 0.0)
        )
        lower_band = factor_above * from_above(lower_band, stride, 0.0)
        upper_band = factor_below * from_below(upper_band, stride, 0.0)
        diagonal = new_diagonal
        source = new_source
        stride = stride * 2
    return source / diagonal


def masked_rates(levels, tracers, coupling, surface):
    blocks, cell_count = surface.shape
    shaped = coupling.reshape(levels, blocks, tracers, cell_count)
    shaped = shaped.at[levels - 1].multiply(surface[:, None, :])
    return shaped.reshape(-1, cell_count)


def interface_values(levels, tracers, profile, surface):
    blocks, cell_count = surface.shape
    shaped = profile.reshape(levels, blocks, tracers, cell_count)
    return shaped[levels - 1, :, :COUPLED] * surface[:, None, :]


def full_interface(tracers, boundary):
    blocks, coupled, cell_count = boundary.shape
    padding = jnp.zeros((blocks, tracers - coupled, cell_count), jnp.float32)
    return jnp.concatenate([boundary, padding], axis=1).reshape(blocks * tracers, cell_count)


def column_solve(levels, tracers, profile, coupling, boundary):
    blocks, coupled, cell_count = boundary.shape
    solved = tridiagonal(
        profile.reshape(levels, blocks * tracers, cell_count),
        coupling.reshape(levels, blocks * tracers, cell_count),
        full_interface(tracers, boundary),
    )
    return solved.reshape(-1, cell_count)


def by_component(is_ocean, function, *operands):
    return lax.cond(
        is_ocean,
        partial(function, LEV_OCN, TRC_OCN),
        partial(function, LEV_ATM, TRC_ATM),
        *operands
    )


def remapped(values, listing, used_count, weights, sections, columns):
    blocks, coupled, cell_count = values.shape
    entries_total = listing.shape[0]
    remapped_items = jnp.einsum(
        "enc,ecd->end", values[listing[:, 0]], weights[listing[:, 2]], precision=highest
    )
    positions = jnp.arange(entries_total, dtype=jnp.int32)
    in_use = positions < used_count
    owner_device = listing[:, 1] // blocks
    local_block = listing[:, 1] % blocks
    peer_count = sections * columns
    earlier_same = (
        (owner_device[:, None] == owner_device[None, :])
        & in_use[None, :]
        & (positions[None, :] < positions[:, None])
    )
    position = jnp.sum(earlier_same.astype(jnp.int32), axis=1)
    slot_index = jnp.where(in_use, owner_device * CAP + position, peer_count * CAP)
    outgoing = (
        jnp.zeros((peer_count * CAP, coupled, cell_count), jnp.float32)
        .at[slot_index]
        .set(remapped_items, mode="drop")
    )
    block_ids = (
        jnp.full((peer_count * CAP,), -1, jnp.int32).at[slot_index].set(local_block, mode="drop")
    )
    incoming, incoming_ids = (
        lax.all_to_all(
            outgoing.reshape(peer_count, CAP, coupled, cell_count),
            ("sec", "col"),
            split_axis=0,
            concat_axis=0,
            tiled=True,
        ),
        lax.all_to_all(
            block_ids.reshape(peer_count, CAP),
            ("sec", "col"),
            split_axis=0,
            concat_axis=0,
            tiled=True,
        ),
    )
    selector = (
        incoming_ids.reshape(-1)[None, :] == jnp.arange(blocks, dtype=jnp.int32)[:, None]
    ).astype(jnp.float32)
    boundary = jnp.dot(selector, incoming.reshape(-1, coupled * cell_count), precision=highest)
    return boundary.reshape(blocks, coupled, cell_count)


def shards(column_state, mixing, surface_mask, pairings, pairing_count, remap_weights):
    sections = lax.axis_size("sec")
    columns = lax.axis_size("col")
    section = lax.axis_index("sec")
    is_ocean = section == sections - 1
    profile = column_state[0]
    cell_count = profile.shape[1]
    surface = surface_mask[0].astype(jnp.float32)
    listing = pairings[0]
    used_count = pairing_count[0, 0]
    weights = remap_weights[0].reshape(-1, cell_count, cell_count)
    coupling = by_component(is_ocean, masked_rates, mixing[0], surface)
    for substep in range(SUBSTEPS):
        values = by_component(is_ocean, interface_values, profile, surface)
        boundary = remapped(values, listing, used_count, weights, sections, columns)
        profile = by_component(is_ocean, column_solve, profile, coupling, boundary)
    return profile[None]


def solution(mesh):
    placed = (
        P("sec", "col", None),
        P("sec", "col", None),
        P("sec", "col", None),
        P("sec", "col", None),
        P("sec", "col"),
        P("sec", "col", None),
    )
    return jax.shard_map(
        shards, mesh=mesh, in_specs=placed, out_specs=P("sec", "col", None), check_vma=False
    )
```

profile of v0, /device:TPU:0, one launch (start us, length us, event | category | flops | bytes accessed | tf_op | source)
XLA Modules:
  0.0 528.6 jit_solution(5698104950562643466)
XLA Ops:
  3.2 11.1 %all-to-all-start = ((s32[128,1,6]{2,1,0:T(1,128)}), s32[128,1,6]{2,1,0:T(1,128)S(1)}, u32[]{:S(2)}, u32[]{:S(2)}) async-start(s32[128,1,6]{2,1,0:T(1,128)} %bitcast.39), calls=%async_computation | async-start | bytes 131072 | tf_op jit(solution)/shard_map/all_to_all | solution.py:133
  15.1 5.2 conditional.6
  15.1 4.4 reshape_squeeze.16
  23.5 5.0 fusion.118
  29.9 6.4 %scatter_fusion = f32[768,4,128]{2,1,0:T(4,128)} fusion(f32[768,4,128]{2,1,0:T(4,128)} %broadcast.737.clone, s32[54]{0:T(128)S(1)} %fusion.21, f32[54,4,128]{2,1,0:T(4,128)S(1)} %fusion.118), kind=kCustom, calls=%fused_computation.4 | custom fusion | bytes 331992 | tf_op jit(solution)/shard_map/scatter | solution.py:120
  36.4 10.3 %all-to-all-start.1 = ((f32[128,6,4,128]{3,2,1,0:T(4,128)}), f32[128,6,4,128]{3,2,1,0:T(4,128)}, u32[]{:S(2)}, u32[]{:S(2)}) async-start(f32[128,6,4,128]{3,2,1,0:T(4,128)} %bitcast.156), calls=%async_computation.1 | async-start | bytes 3145728 | tf_op jit(solution)/shard_map/all_to_all | solution.py:126
  46.7 31.7 %conditional.5 = (f32[5120,128]{1,0:T(8,128)}) conditional(s32[]{:T(128)} %convert_element_type.9, (f32[1,5120,128]{2,1,0:T(8,128)S(1)}, f32[8,128]{1,0:T(8,128)S(1)}) %tuple.265, (f32[1,5120,128]{2,1,0:T(8,128)S(1)}, f32[8,128]{1,0:T(8,128)S(1)}) %tuple.266), branch_computations={%region_0.1_spmd, %region_1.2_spmd} | conditional | flops 8192 | bytes 15826964 | solution.py:91
  47.3 21.1 %reduce.18 = f32[5120,128]{1,0:T(8,128)} reduce(f32[1,5120,128]{2,0,1:T(1,128)S(1)} %bitcast.152, f32[]{:T(128)} %broadcast.777), dimensions={0}, to_apply=%bitcast.reduce_sub_computation.3 | reduce | bytes 5242884 | tf_op jit(solution)/shard_map
  68.4 4.4 reshape_squeeze.14
  73.4 4.5 reshape.323
  82.8 197.7 %conditional.7 = (f32[5120,128]{1,0:T(8,128)}) conditional(s32[]{:T(128)} %convert_element_type.9, (f32[1,5120,128]{2,1,0:T(8,128)}, f32[5120,128]{1,0:T(8,128)}, f32[8,4,128]{2,0,1:T(8,128)S(1)}) %tuple.63, (f32[1,5120,128]{2,1,0:T(8,128)}, f32[5120,128]{1,0:T(8,128)}, f32[8,4,128]{2,0,1:T(8,128)S(1)}) %tuple.63), branch_computations={%region_7.8_spmd, %region_8.9_spmd} | conditional | flops 91745280 | bytes 943378944 | solution.py:91
  101.0 4.4 multiply_add_fusion.10
  112.8 8.7 %multiply_add_fusion.9 = (f32[128,40,128]{2,1,0:T(8,128)}, f32[128,40,128]{2,1,0:T(8,128)S(1)}, f32[128,40,128]{2,1,0:T(8,128)S(1)}) fusion(f32[126,40,128]{2,1,0:T(8,128)} %get-tuple-element.338, f32[128,40,128]{2,1,0:T(8,128)S(1)} %get-tuple-element.283, f32[126,40,128]{2,1,0:T(8,128)} %get-tuple-element.339, f32[126,40,128]{2,1,0:T(8,128)} %get-tuple-element.328, ...), kind=kLoop, calls=%fused_computation.40 | loop fusion | flops 8519680 | bytes 36413440 | tf_op jit(solution)/shard_map/cond/branch_0_fun/add | solution.py:49
  129.4 4.9 multiply_add_fusion.8
  134.3 5.2 fusion.40
  142.3 8.6 %multiply_add_fusion.7 = (f32[128,40,128]{2,1,0:T(8,128)}, f32[128,40,128]{2,1,0:T(8,128)S(1)}, f32[128,40,128]{2,1,0:T(8,128)S(1)}) fusion(f32[124,40,128]{2,1,0:T(8,128)} %get-tuple-element.326, f32[128,40,128]{2,1,0:T(8,128)} %get-tuple-element.232, f32[124,40,128]{2,1,0:T(8,128)} %get-tuple-element.325, f32[124,40,128]{2,1,0:T(8,128)} %get-tuple-element.324, ...), kind=kLoop, calls=%fused_computation.34 | loop fusion | flops 9175040 | bytes 36208640 | tf_op jit(solution)/shard_map/cond/branch_0_fun/add | solution.py:49
  158.6 4.8 multiply_add_fusion.6
  163.4 5.1 fusion.36
  171.3 8.5 %multiply_add_fusion.5 = (f32[128,40,128]{2,1,0:T(8,128)}, f32[128,40,128]{2,1,0:T(8,128)S(1)}, f32[128,40,128]{2,1,0:T(8,128)S(1)}) fusion(f32[120,40,128]{2,1,0:T(8,128)} %get-tuple-element.318, f32[128,40,128]{2,1,0:T(8,128)} %get-tuple-element.229, f32[120,40,128]{2,1,0:T(8,128)} %get-tuple-element.317, f32[120,40,128]{2,1,0:T(8,128)} %get-tuple-element.316, ...), kind=kLoop, calls=%fused_computation.28 | loop fusion | flops 9175040 | bytes 35717120 | tf_op jit(solution)/shard_map/cond/branch_0_fun/add | solution.py:49
  187.5 4.8 multiply_add_fusion.4
  192.2 4.1 fusion.32
  199.9 7.7 %multiply_add_fusion.3 = (f32[128,40,128]{2,1,0:T(8,128)}, f32[128,40,128]{2,1,0:T(8,128)S(1)}, f32[128,40,128]{2,1,0:T(8,128)S(1)}) fusion(f32[112,40,128]{2,1,0:T(8,128)} %get-tuple-element.310, f32[128,40,128]{2,1,0:T(8,128)} %get-tuple-element.226, f32[112,40,128]{2,1,0:T(8,128)} %get-tuple-element.309, f32[112,40,128]{2,1,0:T(8,128)} %get-tuple-element.308, ...), kind=kLoop, calls=%fused_computation.22 | loop fusion | flops 9175040 | bytes 34734080 | tf_op jit(solution)/shard_map/cond/branch_0_fun/add | solution.py:49
  214.8 4.9 multiply_add_fusion.2
  219.7 4.5 fusion.28
  226.4 7.2 %multiply_add_fusion.1 = (f32[128,40,128]{2,1,0:T(8,128)}, f32[128,40,128]{2,1,0:T(8,128)S(1)}, f32[128,40,128]{2,1,0:T(8,128)}) fusion(f32[96,40,128]{2,1,0:T(8,128)} %get-tuple-element.302, f32[128,40,128]{2,1,0:T(8,128)S(1)} %copy-done.90, f32[96,40,128]{2,1,0:T(8,128)} %get-tuple-element.301, f32[96,40,128]{2,1,0:T(8,128)} %get-tuple-element.300, ...), kind=kLoop, calls=%fused_computation.16 | loop fusion | flops 9175040 | bytes 32768000 | tf_op jit(solution)/shard_map/cond/branch_0_fun/add | solution.py:49
  240.3 9.8 %pad_multiply_fusion = (f32[128,40,128]{2,1,0:T(8,128)}, f32[128,40,128]{2,1,0:T(8,128)}, f32[128,40,128]{2,1,0:T(8,128)}) fusion(f32[96,40,128]{2,1,0:T(8,128)} %get-tuple-element.291, f32[96,40,128]{2,1,0:T(8,128)} %get-tuple-element.299, f32[128,40,128]{2,1,0:T(8,128)} %copy-done.94, f32[96,40,128]{2,1,0:T(8,128)} %get-tuple-element.293, ...), kind=kLoop, calls=%fused_computation.13 | loop fusion | flops 6553600 | bytes 27525120 | tf_op jit(solution)/shard_map/cond/branch_0_fun/mul | solution.py:54
  259.3 7.3 %add_divide_fusion = f32[128,40,128]{2,1,0:T(8,128)} fusion(f32[64,40,128]{2,1,0:T(8,128)} %slice.915, f32[128,40,128]{2,1,0:T(8,128)S(1)} %copy-done.105, f32[64,40,128]{2,1,0:T(8,128)} %slice.914, f32[64,40,128]{2,1,0:T(8,128)} %get-tuple-element.290, f32[64,40,128]{2,1,0:T(8,128)} %get-tuple-element.288, f32[128,40,128]{2,1,0:T(8,128)} %get-tuple-element.284, ...), kind=kLoop, calls=%fused_computation.12 | loop fusion | flops 8519680 | bytes 20971520 | tf_op jit(solution)/shard_map/cond/branch_0_fun/div | solution.py:58
  280.5 5.6 %conditional.8 = (f32[8,4,128]{2,1,0:T(4,128)S(1)}) conditional(s32[]{:T(128)} %convert_element_type.9, (f32[5120,128]{1,0:T(8,128)}, f32[8,128]{1,0:T(8,128)}) %tuple.267, (f32[5120,128]{1,0:T(8,128)}, f32[8,128]{1,0:T(8,128)}) %tuple.268), branch_computations={%region_9.10_spmd, %region_10.11_spmd} | conditional | flops 4096 | bytes 5279752 | solution.py:91
  280.5 4.8 reshape.334
  287.4 4.6 fusion.119
  296.2 34.3 %all_to_all.20 = f32[128,6,4,128]{3,2,1,0:T(4,128)S(1)} all-to-all(f32[128,6,4,128]{3,2,1,0:T(4,128)S(1)} %bitcast.155), channel_id=1, replica_groups=mesh['sec'=4,'col'=32] {'sec','col'}, dimensions={0} | all-to-all | bytes 3145728 | tf_op jit(solution)/shard_map/all_to_all | solution.py:126
  332.0 194.8 %conditional.9 = (f32[1,5120,128]{2,1,0:T(8,128)}) conditional(s32[]{:T(128)} %convert_element_type.9, (f32[5120,128]{1,0:T(8,128)}, f32[5120,128]{1,0:T(8,128)}, f32[8,4,128]{2,0,1:T(8,128)S(1)}) %tuple.65, (f32[5120,128]{1,0:T(8,128)}, f32[5120,128]{1,0:T(8,128)}, f32[8,4,128]{2,0,1:T(8,128)S(1)}) %tuple.65), branch_computations={%region_12.13_spmd, %region_13.14_spmd} | conditional | flops 91745280 | bytes 932893184 | solution.py:91
  352.0 4.6 multiply_add_fusion.34
  356.7 4.2 fusion.90
  364.0 8.7 %multiply_add_fusion.33 = (f32[128,40,128]{2,1,0:T(8,128)}, f32[128,40,128]{2,1,0:T(8,128)S(1)}, f32[128,40,128]{2,1,0:T(8,128)S(1)}) fusion(f32[126,40,128]{2,1,0:T(8,128)} %get-tuple-element.454, f32[128,40,128]{2,1,0:T(8,128)S(1)} %get-tuple-element.399, f32[126,40,128]{2,1,0:T(8,128)} %get-tuple-element.455, f32[126,40,128]{2,1,0:T(8,128)} %get-tuple-element.444, ...), kind=kLoop, calls=%fused_computation.131 | loop fusion | flops 8519680 | bytes 36413440 | tf_op jit(solution)/shard_map/cond/branch_0_fun/add | solution.py:49
  380.6 4.9 multiply_add_fusion.32
  385.4 5.4 %fusion.88 = (f32[124,40,128]{2,1,0:T(8,128)}, f32[124,40,128]{2,1,0:T(8,128)}) fusion(f32[128,40,128]{2,1,0:T(8,128)} %multiply_add_fusion.32), kind=kLoop, calls=%fused_computation.293 | loop fusion | bytes 10158080 | tf_op jit(solution)/shard_map/cond/branch_0_fun/slice | solution.py:27
  393.6 8.6 %multiply_add_fusion.31 = (f32[128,40,128]{2,1,0:T(8,128)}, f32[128,40,128]{2,1,0:T(8,128)S(1)}, f32[128,40,128]{2,1,0:T(8,128)S(1)}) fusion(f32[124,40,128]{2,1,0:T(8,128)} %get-tuple-element.442, f32[128,40,128]{2,1,0:T(8,128)} %get-tuple-element.262, f32[124,40,128]{2,1,0:T(8,128)} %get-tuple-element.441, f32[124,40,128]{2,1,0:T(8,128)} %get-tuple-element.440, ...), kind=kLoop, calls=%fused_computation.125 | loop fusion | flops 9175040 | bytes 36208640 | tf_op jit(solution)/shard_map/cond/branch_0_fun/add | solution.py:49
  409.9 4.8 multiply_add_fusion.30
  414.8 5.1 fusion.84
  422.7 8.5 %multiply_add_fusion.29 = (f32[128,40,128]{2,1,0:T(8,128)}, f32[128,40,128]{2,1,0:T(8,128)S(1)}, f32[128,40,128]{2,1,0:T(8,128)S(1)}) fusion(f32[120,40,128]{2,1,0:T(8,128)} %get-tuple-element.434, f32[128,40,128]{2,1,0:T(8,128)} %get-tuple-element.259, f32[120,40,128]{2,1,0:T(8,128)} %get-tuple-element.433, f32[120,40,128]{2,1,0:T(8,128)} %get-tuple-element.432, ...), kind=kLoop, calls=%fused_computation.119 | loop fusion | flops 9175040 | bytes 35717120 | tf_op jit(solution)/shard_map/cond/branch_0_fun/add | solution.py:49
  438.7 4.8 multiply_add_fusion.28
  451.2 7.7 %multiply_add_fusion.27 = (f32[128,40,128]{2,1,0:T(8,128)}, f32[128,40,128]{2,1,0:T(8,128)S(1)}, f32[128,40,128]{2,1,0:T(8,128)S(1)}) fusion(f32[112,40,128]{2,1,0:T(8,128)} %get-tuple-element.426, f32[128,40,128]{2,1,0:T(8,128)} %get-tuple-element.256, f32[112,40,128]{2,1,0:T(8,128)} %get-tuple-element.425, f32[112,40,128]{2,1,0:T(8,128)} %get-tuple-element.424, ...), kind=kLoop, calls=%fused_computation.113 | loop fusion | flops 9175040 | bytes 34734080 | tf_op jit(solution)/shard_map/cond/branch_0_fun/add | solution.py:49
  466.1 4.9 multiply_add_fusion.26
  471.0 4.5 fusion.76
  477.7 7.2 %multiply_add_fusion.25 = (f32[128,40,128]{2,1,0:T(8,128)}, f32[128,40,128]{2,1,0:T(8,128)S(1)}, f32[128,40,128]{2,1,0:T(8,128)}) fusion(f32[96,40,128]{2,1,0:T(8,128)} %get-tuple-element.418, f32[128,40,128]{2,1,0:T(8,128)S(1)} %copy-done.91, f32[96,40,128]{2,1,0:T(8,128)} %get-tuple-element.417, f32[96,40,128]{2,1,0:T(8,128)} %get-tuple-element.416, ...), kind=kLoop, calls=%fused_computation.107 | loop fusion | flops 9175040 | bytes 32768000 | tf_op jit(solution)/shard_map/cond/branch_0_fun/add | solution.py:49
  491.6 9.8 %pad_multiply_fusion.24 = (f32[128,40,128]{2,1,0:T(8,128)}, f32[128,40,128]{2,1,0:T(8,128)}, f32[128,40,128]{2,1,0:T(8,128)}) fusion(f32[96,40,128]{2,1,0:T(8,128)} %get-tuple-element.407, f32[96,40,128]{2,1,0:T(8,128)} %get-tuple-element.415, f32[128,40,128]{2,1,0:T(8,128)} %copy-done.96, f32[96,40,128]{2,1,0:T(8,128)} %get-tuple-element.409, ...), kind=kLoop, calls=%fused_computation.104 | loop fusion | flops 6553600 | bytes 27525120 | tf_op jit(solution)/shard_map/cond/branch_0_fun/mul | solution.py:54
  510.6 7.3 %add_divide_fusion.2 = f32[128,40,128]{2,1,0:T(8,128)} fusion(f32[64,40,128]{2,1,0:T(8,128)} %slice.1019, f32[128,40,128]{2,1,0:T(8,128)S(1)} %copy-done.106, f32[64,40,128]{2,1,0:T(8,128)} %slice.1018, f32[64,40,128]{2,1,0:T(8,128)} %get-tuple-element.406, f32[64,40,128]{2,1,0:T(8,128)} %get-tuple-element.404, f32[128,40,128]{2,1,0:T(8,128)} %get-tuple-element.400, ...), kind=kLoop, calls=%fused_computation.103 | loop fusion | flops 8519680 | bytes 20971520 | tf_op jit(solution)/shard_map/cond/branch_0_fun/div | solution.py:58
  (247 shorter events, 190.9 us)
Async XLA Ops:
  0.0 20.9 %copy-start = (f32[1,2048,128]{2,1,0:T(8,128)S(1)}, f32[1,2048,128]{2,1,0:T(8,128)}, u32[]{:S(2)}) copy-start(f32[1,2048,128]{2,1,0:T(8,128)} %param.33) | copy-start | bytes 3145732
  1.7 28.2 %copy-start.131 = (s32[54]{0:T(128)}, s32[54]{0:T(128)S(1)}, u32[]{:S(2)}) copy-start(s32[54]{0:T(128)S(1)} %fusion.21) | copy-start | bytes 652
  3.2 33.2 %all-to-all-start = ((s32[128,1,6]{2,1,0:T(1,128)}), s32[128,1,6]{2,1,0:T(1,128)S(1)}, u32[]{:S(2)}, u32[]{:S(2)}) async-start(s32[128,1,6]{2,1,0:T(1,128)} %bitcast.39), calls=%async_computation | async-start | bytes 131072 | tf_op jit(solution)/shard_map/all_to_all | solution.py:133
  15.1 31.7 %copy-start.123 = (f32[8,128]{1,0:T(8,128)}, f32[8,128]{1,0:T(8,128)S(1)}, u32[]{:S(2)}) copy-start(f32[8,128]{1,0:T(8,128)S(1)} %convert_bitcast_fusion) | copy-start | bytes 12292
  15.1 5.2 copy-start.130
  28.5 18.2 %copy-start.121 = (f32[1,5120,128]{2,1,0:T(8,128)S(1)}, f32[1,5120,128]{2,1,0:T(8,128)}, u32[]{:S(2)}) copy-start(f32[1,5120,128]{2,1,0:T(8,128)} %param.29) | copy-start | bytes 7864324
  36.4 43.6 %all-to-all-start.1 = ((f32[128,6,4,128]{3,2,1,0:T(4,128)}), f32[128,6,4,128]{3,2,1,0:T(4,128)}, u32[]{:S(2)}, u32[]{:S(2)}) async-start(f32[128,6,4,128]{3,2,1,0:T(4,128)} %bitcast.156), calls=%async_computation.1 | async-start | bytes 3145728 | tf_op jit(solution)/shard_map/all_to_all | solution.py:126
  89.8 3.4 copy-start.101
  96.2 3.3 copy-start.3
  96.2 4.1 copy-start.6
  96.2 4.9 copy-start.8
  105.5 4.7 copy-start.10
  124.2 4.4 copy-start.15
  124.2 5.2 copy-start.16
  134.3 5.2 copy-start.32
  153.5 4.3 copy-start.36
  153.5 5.1 copy-start.37
  163.4 5.1 copy-start.50
  182.5 4.3 copy-start.54
  182.5 5.0 copy-start.55
  192.2 4.2 copy-start.68
  196.4 3.5 copy-start.56
  210.0 4.1 copy-start.73
  210.0 4.8 copy-start.74
  219.7 4.5 copy-start.90
  233.6 3.6 copy-start.95
  253.3 3.4 copy-start.103
  280.4 7.0 %copy-start.98 = (f32[54,128,128]{2,1,0:T(8,128)S(1)}, f32[54,128,128]{2,1,0:T(8,128)}, u32[]{:S(2)}) copy-start(f32[54,128,128]{2,1,0:T(8,128)} %gather_fusion.1) | copy-start | bytes 10616836
  287.4 4.8 copy-start.132
  347.2 3.3 copy-start.5
  347.2 4.1 copy-start.7
  347.2 4.9 copy-start.9
  356.7 4.7 copy-start.12
  375.4 4.4 copy-start.19
  375.4 5.2 copy-start.20
  385.4 5.4 %copy-start.33 = (f32[128,40,128]{2,1,0:T(8,128)S(1)}, f32[128,40,128]{2,1,0:T(8,128)}, u32[]{:S(2)}) copy-start(f32[128,40,128]{2,1,0:T(8,128)} %get-tuple-element.262) | copy-start | bytes 7864324 | tf_op jit(solution)/shard_map/cond
  404.8 4.3 copy-start.39
  404.8 5.1 copy-start.40
  414.8 5.1 copy-start.51
  433.7 4.3 copy-start.57
  433.7 5.0 copy-start.58
  443.5 4.2 copy-start.69
  447.7 3.5 copy-start.59
  461.3 4.1 copy-start.76
  461.3 4.8 copy-start.77
  471.0 4.5 copy-start.91
  484.9 3.6 copy-start.97
  504.6 3.3 copy-start.104
  (31 other events, 84.6 us)
where the time goes:
time: 539 us; the launch traced here: 529 us
  local copies, waits for them, and re-layouts  235 us (44%)
  other arithmetic  202 us (37%)
  blocking collectives  34.3 us (6%)
  loops' own time  23.5 us (4%)
  starting transfers between devices  21.5 us (4%)
  matrix products  11.3 us (2%)
    slice x26, local copies, waits for them, and re-layouts, from_below(): return jnp.concatenate([field[stride:], tail], axis=0)  83.4 us
    add x10, other arithmetic, tridiagonal(): source + factor_above * from_above(source, stride, 0.0)  81.5 us
    slice x26, local copies, waits for them, and re-layouts, from_above(): return jnp.concatenate([head, field[:-stride]], axis=0)  64.2 us
    add x10, other arithmetic, tridiagonal(): diagonal + factor_above * from_above(upper_band, stride, 0.0)  47.9 us
    cond x136, local copies, waits for them, and re-layouts  41.1 us
    all_to_all x1, blocking collectives, remapped(): lax.all_to_all(outgoing.reshape(peer_count, CAP, coupled, cell_count), ('...  34.3 us
    another operation x5, loops' own time, by_component(): lax.cond(is_ocean, partial(function, LEV_OCN, TRC_OCN), partial(function,...  23.5 us
    another operation x1, other arithmetic  21.1 us
  transfers between devices with their start and end apart: 2, of which 0 were waited for; matrix products, arithmetic and copies ran while one was open for 10% of the time, Pallas kernels for 0%

commit v1 on v0

v1 whole, which is shorter than its diff:
```python
from functools import partial

import jax
import jax.numpy as jnp
from jax import lax
from jax.experimental import pallas as pl
from jax.experimental.pallas import tpu as pltpu
from jax.sharding import PartitionSpec as P

CELLS = 128
LEV_ATM = 128
LEV_OCN = 80
TRC_ATM = 5
TRC_OCN = 8
COUPLED = 4
BLK = 8
WBLK = 16
ROWS = 5120
WIDE = BLK * COUPLED
CHUNK = 320
CHUNKS = ROWS // CHUNK
SECS = 4
ROTATIONS = SECS - 1
SPAN = ROTATIONS * WIDE

f32 = jnp.float32
bf16 = jnp.bfloat16
MIB = 1 << 20

ATM = (LEV_ATM, TRC_ATM)
OCN = (LEV_OCN, TRC_OCN)


def vmem():
    return pl.BlockSpec(memory_space=pltpu.VMEM)


def smem():
    return pl.BlockSpec(memory_space=pltpu.SMEM)


def anywhere():
    return pl.BlockSpec(memory_space=pl.ANY)


def call(kernel, outs, in_specs, scratch, limit, flops, nbytes, out_specs=None):
    return pl.pallas_call(
        kernel,
        out_shape=[jax.ShapeDtypeStruct(shape, kind) for shape, kind in outs],
        in_specs=in_specs,
        out_specs=out_specs or [vmem()] * len(outs),
        scratch_shapes=scratch,
        compiler_params=pltpu.CompilerParams(vmem_limit_bytes=limit * MIB),
        cost_estimate=pl.CostEstimate(flops=flops, bytes_accessed=nbytes, transcendentals=0),
    )


def per_component(body):
    ocean = lax.axis_index("sec") == SECS - 1
    pl.when(ocean)(partial(body, *OCN))
    pl.when(jnp.logical_not(ocean))(partial(body, *ATM))


def compact(tracers, rows):
    return jnp.concatenate(
        [rows[b * tracers : b * tracers + COUPLED] for b in range(BLK)], axis=0
    )


def spread(tracers, values, target):
    for b in range(BLK):
        target[b * tracers : b * tracers + COUPLED] = values[b * COUPLED : (b + 1) * COUPLED]
        rest = tracers - COUPLED
        target[b * tracers + COUPLED : (b + 1) * tracers] = jnp.zeros((rest, CELLS), f32)


def by_field(mask, fields):
    return jnp.concatenate(
        [jnp.broadcast_to(mask[b : b + 1], (fields, CELLS)) for b in range(BLK)], axis=0
    )


def send_products(surface, high, low, listing, count, products, own, near, far):
    part_high = surface.astype(bf16)
    part_low = (surface - part_high.astype(f32)).astype(bf16)
    left = jnp.concatenate([part_high, part_low], axis=0)
    for w in range(WBLK):
        rows = slice(w * CELLS, (w + 1) * CELLS)
        both = jnp.dot(left, high[rows], preferred_element_type=f32) + jnp.dot(
            left, low[rows], preferred_element_type=f32
        )
        products[w * BLK : (w + 1) * BLK] = (both[:WIDE] + both[WIDE:]).reshape(
            BLK, COUPLED, CELLS
        )
    for target in (own, near, far):
        target[...] = jnp.zeros_like(target)
    sec = lax.axis_index("sec")
    col = lax.axis_index("col")
    columns = lax.axis_size("col")

    def entry(e, carry):
        source = listing[e, 0]
        goal = listing[e, 1]
        weight = listing[e, 2]
        block = lax.rem(goal, BLK)
        device = lax.div(goal, BLK)
        to_col = lax.rem(device, columns)
        to_sec = lax.div(device, columns)
        slot = lax.rem(to_sec - sec + (SECS - 1), SECS) * BLK + block
        piece = products[weight * BLK + lax.rem(source, BLK)]
        same = to_col == col
        beside = to_col == jnp.bitwise_xor(col, 1)

        @pl.when(same)
        def _():
            own[slot] += piece

        @pl.when(beside)
        def _():
            near[slot] += piece

        @pl.when(jnp.logical_not(jnp.logical_or(same, beside)))
        def _():
            far[slot] += piece

        return carry

    lax.fori_loop(0, count[0, 0], entry, 0)


def first_kernel(tail, mask, listing, count, weights, own, near, far, high, low, top, products):
    source_cell = mask[...].astype(f32)
    split = weights[...].astype(bf16)
    high[...] = split
    low[...] = (weights[...] - split.astype(f32)).astype(bf16)

    def component(levels, tracers):
        width = BLK * tracers
        top[...] = compact(tracers, tail[tail.shape[0] - width :])

    per_component(component)
    surface = top[...] * by_field(source_cell, COUPLED)
    send_products(surface, high, low, listing, count, products, own, near, far)


def middle_kernel(
    got1, got2, got3, c_tail, d_tail, mask, listing, count, high, low, boundary, own, near, far, top, products
):
    source_cell = mask[...].astype(f32)
    arrived = got1[...] + got2[...] + got3[...]
    boundary[...] = arrived

    def component(levels, tracers):
        width = BLK * tracers
        start = c_tail.shape[0] - width
        top[...] = compact(tracers, d_tail[start:]) + compact(tracers, c_tail[start:]) * arrived

    per_component(component)
    surface = top[...] * by_field(source_cell, COUPLED)
    send_products(surface, high, low, listing, count, products, own, near, far)


def eliminate_kernel(state, mixing, mask, c, d, w, e, s_buf, r_buf, sems):
    def copies(i):
        rows = pl.ds(pl.multiple_of(i * CHUNK, CHUNK), CHUNK)
        return (
            pltpu.make_async_copy(state.at[rows], s_buf.at[rows], sems.at[0, i]),
            pltpu.make_async_copy(mixing.at[rows], r_buf.at[rows], sems.at[1, i]),
        )

    for i in range(CHUNKS):
        for copy in copies(i):
            copy.start()
    source_cell = mask[...].astype(f32)

    def component(levels, tracers):
        width = BLK * tracers
        per_chunk = CHUNK // width

        def chunk(i, carry):
            for copy in copies(i):
                copy.wait()

            @pl.when(i == CHUNKS - 1)
            def _():
                r_buf[ROWS - width :] *= by_field(source_cell, tracers)

            r_above, c_above, d_above = carry
            for j in range(per_chunk):
                rows = pl.ds(pl.multiple_of(i * CHUNK + j * width, 8), width)
                r = r_buf[rows]
                inverse = 1.0 / (1.0 + r + r_above * (1.0 - c_above))
                lower = r_above * inverse
                c_above = r * inverse
                d_above = s_buf[rows] * inverse + lower * d_above
                w[rows] = inverse
                e[rows] = lower
                c[rows] = c_above
                d[rows] = d_above
                r_above = r
            return r_above, c_above, d_above

        zero = jnp.zeros((width, CELLS), f32)
        lax.fori_loop(0, CHUNKS, chunk, (zero, zero, zero))

    per_component(component)


def substitute_kernel(c, d, y, g):
    def component(levels, tracers):
        width = BLK * tracers
        per_chunk = CHUNK // width

        def chunk(i, carry):
            y_below, g_below = carry
            for j in range(per_chunk):
                rows = pl.ds(pl.multiple_of(ROWS - i * CHUNK - (j + 1) * width, 8), width)
                upper = c[rows]
                y_below = d[rows] + upper * y_below
                g_below = upper * g_below
                y[rows] = y_below
                g[rows] = g_below
            return y_below, g_below

        zero = jnp.zeros((width, CELLS), f32)
        lax.fori_loop(0, CHUNKS, chunk, (zero, jnp.ones_like(zero)))

    per_component(component)


def again_kernel(boundary, y, g, w, e, c, u, wide):
    def component(levels, tracers):
        width = BLK * tracers
        per_chunk = CHUNK // width
        spread(tracers, boundary[...], wide)

        def down(i, d_above):
            b = wide[:width]
            for j in range(per_chunk):
                rows = pl.ds(pl.multiple_of(i * CHUNK + j * width, 8), width)
                d_above = (y[rows] + b * g[rows]) * w[rows] + e[rows] * d_above
                u[rows] = d_above
            return d_above

        def up(i, below):
            for j in range(per_chunk):
                rows = pl.ds(pl.multiple_of(ROWS - i * CHUNK - (j + 1) * width, 8), width)
                below = u[rows] + c[rows] * below
                u[rows] = below
            return below

        zero = jnp.zeros((width, CELLS), f32)
        lax.fori_loop(0, CHUNKS, down, zero)
        lax.fori_loop(0, CHUNKS, up, zero)

    per_component(component)


def finish_kernel(got1, got2, got3, u, g, out, wide, buf, sems):
    arrived = got1[...] + got2[...] + got3[...]

    def copy(i):
        rows = pl.ds(pl.multiple_of(i * CHUNK, CHUNK), CHUNK)
        return pltpu.make_async_copy(buf.at[rows], out.at[rows], sems.at[i])

    def component(levels, tracers):
        width = BLK * tracers
        per_chunk = CHUNK // width
        spread(tracers, arrived, wide)

        def chunk(i, carry):
            b = wide[:width]
            for j in range(per_chunk):
                rows = pl.ds(pl.multiple_of(i * CHUNK + j * width, 8), width)
                buf[rows] = u[rows] + b * g[rows]
            copy(i).start()
            return carry

        lax.fori_loop(0, CHUNKS, chunk, 0)

    per_component(component)

    def finish(i, carry):
        copy(i).wait()
        return carry

    lax.fori_loop(0, CHUNKS, finish, 0)


def rotations(mesh_shape):
    secs, cols = mesh_shape
    every = [(s, c) for s in range(secs) for c in range(cols)]

    def table(move):
        result = []
        for s, c in every:
            to_s, to_c = move(s, c)
            result.append((s * cols + c, (to_s % secs) * cols + to_c % cols))
        return result

    near = table(lambda s, c: (s, c ^ 1))
    far = table(lambda s, c: (s, c + 1 if c % 2 else c - 1))
    turns = [table(lambda s, c, k=k: (s + k, c)) for k in range(1, secs)]
    return near, far, turns


AXES = ("sec", "col")


def exchange(own, near, far, tables):
    to_near, to_far, turns = tables
    from_far = lax.ppermute(far, AXES, to_far)
    from_near = lax.ppermute(near, AXES, to_near)
    total = own + from_near + from_far
    return [
        lax.ppermute(total[k * BLK : (k + 1) * BLK], AXES, turns[k]).reshape(WIDE, CELLS)
        for k in range(ROTATIONS)
    ]


def shards(column_state, mixing, surface_mask, pairings, pairing_count, remap_weights):
    tables = rotations((lax.axis_size("sec"), lax.axis_size("col")))
    state = column_state[0]
    rates = mixing[0]
    mask = surface_mask[0]
    listing = pairings[0]
    weights = remap_weights[0]
    full = (ROWS, CELLS)
    payload = ((ROTATIONS * BLK, COUPLED, CELLS), f32)
    half = ((WBLK * CELLS, CELLS), bf16)
    tail = 64
    products = pltpu.VMEM((WBLK * BLK, COUPLED, CELLS), f32)
    top = pltpu.VMEM((WIDE, CELLS), f32)
    wide = pltpu.VMEM((tail, CELLS), f32)
    last = pl.BlockSpec((tail, CELLS), lambda i: (ROWS // tail - 1, 0))

    def whole(shape):
        return pl.BlockSpec(shape, lambda i: (0,) * len(shape))

    own, near, far, high, low = pl.pallas_call(
        first_kernel,
        out_shape=[jax.ShapeDtypeStruct(*spec) for spec in (payload, payload, payload, half, half)],
        grid=(1,),
        in_specs=[last, whole(mask.shape), smem(), smem(), whole(weights.shape)],
        out_specs=[whole(payload[0])] * 3 + [whole(half[0])] * 2,
        scratch_shapes=[top, products],
        compiler_params=pltpu.CompilerParams(vmem_limit_bytes=8 * MIB),
    )(state, mask, listing, pairing_count, weights)

    c, d, w, e = call(
        eliminate_kernel,
        [(full, f32)] * 4,
        [anywhere(), anywhere(), vmem()],
        [pltpu.VMEM(full, f32), pltpu.VMEM(full, f32), pltpu.SemaphoreType.DMA((2, CHUNKS))],
        8,
        20 * ROWS * CELLS,
        6 * ROWS * CELLS * 4,
    )(state, rates, mask)
    y, g = call(
        substitute_kernel, [(full, f32)] * 2, [vmem()] * 2, [], 2, 4 * ROWS * CELLS, 4 * ROWS * CELLS * 4
    )(c, d)

    got = exchange(own, near, far, tables)

    boundary, own, near, far = pl.pallas_call(
        middle_kernel,
        out_shape=[jax.ShapeDtypeStruct(*spec) for spec in (((WIDE, CELLS), f32), payload, payload, payload)],
        grid=(1,),
        in_specs=[whole((WIDE, CELLS))] * 3
        + [last, last, whole(mask.shape), smem(), smem()]
        + [whole(half[0])] * 2,
        out_specs=[whole((WIDE, CELLS))] + [whole(payload[0])] * 3,
        scratch_shapes=[top, products],
        compiler_params=pltpu.CompilerParams(vmem_limit_bytes=8 * MIB),
    )(*got, c, d, mask, listing, pairing_count, high, low)

    (u,) = call(
        again_kernel,
        [(full, f32)],
        [vmem()] * 6,
        [wide],
        2,
        6 * ROWS * CELLS,
        9 * ROWS * CELLS * 4,
    )(boundary, y, g, w, e, c)

    got = exchange(own, near, far, tables)

    (out,) = call(
        finish_kernel,
        [(full, f32)],
        [vmem()] * 5,
        [wide, pltpu.VMEM(full, f32), pltpu.SemaphoreType.DMA((CHUNKS,))],
        5,
        2 * ROWS * CELLS,
        3 * ROWS * CELLS * 4,
        [anywhere()],
    )(*got, u, g)
    return out[None]


def solution(mesh):
    placed = (
        P("sec", "col", None),
        P("sec", "col", None),
        P("sec", "col", None),
        P("sec", "col", None),
        P("sec", "col"),
        P("sec", "col", None),
    )
    return jax.shard_map(
        shards, mesh=mesh, in_specs=placed, out_specs=P("sec", "col", None), check_vma=False
    )
```

time: 539 us -> 51.1 us (0.09); the launches traced: 529 us -> 50.7 us
  local copies, waits for them, and re-layouts: 235 us -> 6.19 us
  other arithmetic: 202 us -> 0.02 us
  blocking collectives: 34.3 us -> 0 us
  loops' own time: 23.5 us -> 0 us
  Pallas kernels: 0 us -> 15.8 us
  matrix products: 11.3 us -> 0 us
  waiting for transfers between devices: 0.01 us -> 7.21 us
    slice x54 -> x2, local copies, waits for them, and re-layouts: 151 us -> 0.01 us  [exchange(): total[k * BLK:(k + 1) * BLK]]
    add x22 -> x2, other arithmetic: 133 us -> 0.02 us  [exchange(): total = own + from_near + from_far]
    cond x136 -> x0, local copies, waits for them, and re-layouts: 41.1 us -> none
    all_to_all x1 -> x0, blocking collectives: 34.3 us -> none  [remapped(): lax.all_to_all(outgoing.reshape(peer_count, CAP, coupled, cell_count), ('...]
    another operation x5 -> x0, loops' own time: 23.5 us -> none  [by_component(): lax.cond(is_ocean, partial(function, LEV_OCN, TRC_OCN), partial(function,...]
    another operation x2 -> x0, other arithmetic: 21.8 us -> none
    all_to_all x2 -> x0, starting transfers between devices: 21.5 us -> none  [the longest x1 11.1 us: remapped(): lax.all_to_all(block_ids.reshape(peer_count, CAP), ('sec', 'col'), split_...]
    mul x4 -> x0, other arithmetic: 21.2 us -> none  [the longest x2 19.7 us: tridiagonal(): upper_band = factor_below * from_below(upper_band, stride, 0.0)]
  transfers between devices with their start and end apart: 2 -> 10, of which waited for: 0 -> 4; matrix products, arithmetic and copies ran while one was open for 10% -> 0% of each run, Pallas kernels for 0% -> 20%
where the time goes in v1:
time: 51.1 us; the launch traced here: 50.7 us
  starting transfers between devices  20.7 us (41%)
  Pallas kernels  15.8 us (31%)
  waiting for transfers between devices  7.21 us (14%)
  local copies, waits for them, and re-layouts  6.19 us (12%)
  between operations  0.78 us (2%)
    ppermute x2, starting transfers between devices, exchange(): from_far = lax.ppermute(far, AXES, to_far)  11 us
    ppermute x6, starting transfers between devices, exchange(): lax.ppermute(total[k * BLK:(k + 1) * BLK], AXES, turns[k])  9.57 us
    pallas_call x1, Pallas kernels, shards(): call(eliminate_kernel, [(full, f32)] * 4, [anywhere(), anywhere(), vmem()...  8.47 us
    unnamed x13, local copies, waits for them, and re-layouts  6.18 us
    ppermute x2, waiting for transfers between devices, exchange(): from_far = lax.ppermute(far, AXES, to_far)  4.06 us
    ppermute x6, waiting for transfers between devices, exchange(): lax.ppermute(total[k * BLK:(k + 1) * BLK], AXES, turns[k])  3.14 us
    pallas_call x1, Pallas kernels, shards(): pl.pallas_call(first_kernel, out_shape=[jax.ShapeDtypeStruct(*spec) for s...  1.99 us
    pallas_call x1, Pallas kernels, shards(): pl.pallas_call(middle_kernel, out_shape=[jax.ShapeDtypeStruct(*spec) for...  1.88 us
  transfers between devices with their start and end apart: 10, of which 4 were waited for; matrix products, arithmetic and copies ran while one was open for 0% of the time, Pallas kernels for 20%

profile of v1, /device:TPU:0, one launch (start us, length us, event | category | flops | bytes accessed | tf_op | source)
XLA Modules:
  0.0 50.7 jit_solution(12422738866559383653)
XLA Ops:
  0.0 0.0 copy-start.5
  0.7 0.8 %copy.7 = s32[1,54,3]{2,1,0:T(8,128)S(1)} copy(s32[1,54,3]{1,0,2:T(1,128)} %param.9) | data formatting | bytes 1296 | tf_op args[3]
  1.4 0.0 copy-start
  1.5 1.7 %copy-done = f32[1,5120,128]{2,1,0:T(8,128)S(1)} copy-done((f32[1,5120,128]{2,1,0:T(8,128)S(1)}, f32[1,5120,128]{2,1,0:T(8,128)}, u32[]{:S(2)}) %copy-start) | copy-done | bytes 2621464
  3.2 0.0 copy-start.3
  3.2 1.2 %copy-done.3 = f32[1,2048,128]{2,1,0:T(8,128)S(1)} copy-done((f32[1,2048,128]{2,1,0:T(8,128)S(1)}, f32[1,2048,128]{2,1,0:T(8,128)}, u32[]{:S(2)}) %copy-start.3) | copy-done | bytes 1048600
  4.4 0.0 copy-start.4
  4.4 0.7 %copy-done.4 = s32[1,8,128]{2,1,0:T(8,128)S(1)} copy-done((s32[1,8,128]{2,1,0:T(8,128)S(1)}, s32[1,8,128]{2,1,0:T(8,128)}, u32[]{:S(2)}) %copy-start.4) | copy-done | bytes 4120
  5.1 0.0 copy-start.1
  5.1 2.0 %shard_map.64 = (f32[24,4,128]{2,1,0:T(4,128)S(1)}, f32[24,4,128]{2,1,0:T(4,128)S(1)}, f32[24,4,128]{2,1,0:T(4,128)S(1)}, bf16[2048,128]{1,0:T(8,128)(2,1)S(1)}, bf16[2048,128]{1,0:T(8,128)(2,1)S(1)}) custom-call(f32[5120,128]{1,0:T(8,128)S(1)} %bitcast.20, s32[8,128]{1,0:T(8,128)S(1)} %bitcast.28, s32[54,3]{1,0:T(8,128)S(1)} %bitcast.24, ...), custom_call_target="tpu_custom_call" | custom-call | tf_op jit(solution)/shard_map/pallas_call | solution.py:340
  7.1 0.1 collective-permute-start
  7.2 6.4 %collective-permute-start.1 = (f32[24,4,128]{2,1,0:T(4,128)S(1)}, f32[24,4,128]{2,1,0:T(4,128)S(1)}, u32[]{:S(2)}, u32[]{:S(2)}) collective-permute-start(f32[24,4,128]{2,1,0:T(4,128)S(1)} %get-tuple-element.22), channel_id=1, source_target_pairs={{0,31},{1,2},{2,1},{3,4},{4,3},{5,6},{6,5},{7,8},{8,7},{9,10},{10,... | collective-permute-start | bytes 147464 | tf_op jit(solution)/shard_map/ppermute | solution.py:312
  13.6 0.0 collective-permute-done
  13.6 1.8 %collective-permute-done.1 = f32[24,4,128]{2,1,0:T(4,128)S(1)} collective-permute-done((f32[24,4,128]{2,1,0:T(4,128)S(1)}, f32[24,4,128]{2,1,0:T(4,128)S(1)}, u32[]{:S(2)}, u32[]{:S(2)}) %collective-permute-start.1) | collective-permute-done | bytes 49184 | tf_op jit(solution)/shard_map/ppermute | solution.py:312
  15.4 3.9 %collective-permute-start.4 = (f32[8,4,128]{2,1,0:T(4,128)S(1)}, f32[8,4,128]{2,1,0:T(4,128)S(1)}, u32[]{:S(2)}, u32[]{:S(2)}) collective-permute-start(f32[8,4,128]{2,1,0:T(4,128)S(1)} %get-tuple-element.38), channel_id=1, source_target_pairs={{0,96},{1,97},{2,98},{3,99},{4,100},{5,101},{6,102},{7,103},{8,104... | collective-permute-start | bytes 49160 | tf_op jit(solution)/shard_map/ppermute | solution.py:316
  19.3 0.0 collective-permute-start.3
  19.3 0.9 %collective-permute-start.2 = (f32[8,4,128]{2,1,0:T(4,128)S(1)}, f32[8,4,128]{2,1,0:T(4,128)S(1)}, u32[]{:S(2)}, u32[]{:S(2)}) collective-permute-start(f32[8,4,128]{2,1,0:T(4,128)S(1)} %get-tuple-element.40), channel_id=1, source_target_pairs={{0,32},{1,33},{2,34},{3,35},{4,36},{5,37},{6,38},{7,39},{8,40},{9,... | collective-permute-start | bytes 49160 | tf_op jit(solution)/shard_map/ppermute | solution.py:316
  20.3 0.0 copy-done.5
  20.3 0.0 copy-done.1
  20.3 0.0 copy-start.2
  20.3 1.7 %copy-done.2 = f32[1,5120,128]{2,1,0:T(8,128)S(1)} copy-done((f32[1,5120,128]{2,1,0:T(8,128)S(1)}, f32[1,5120,128]{2,1,0:T(8,128)}, u32[]{:S(2)}) %copy-start.2) | copy-done | bytes 2621464
  22.0 8.5 %shard_map.65 = (f32[5120,128]{1,0:T(8,128)S(1)}, f32[5120,128]{1,0:T(8,128)S(1)}, f32[5120,128]{1,0:T(8,128)S(1)}, f32[5120,128]{1,0:T(8,128)S(1)}) custom-call(f32[5120,128]{1,0:T(8,128)S(1)} %bitcast.21, f32[5120,128]{1,0:T(8,128)S(1)} %bitcast.22, s32[8,128]{1,0:T(8,128)S(1)} %bitcast.29), custom_call_target="tpu_custom_call" | custom-call | flops 13107200 | bytes 15728640 | tf_op jit(solution)/shard_map/pallas_call | solution.py:350
  30.5 0.0 collective-permute-done.4
  30.5 0.0 collective-permute-done.3
  30.5 0.0 collective-permute-done.2
  30.5 1.9 %shard_map.66 = (f32[32,128]{1,0:T(8,128)S(1)}, f32[24,4,128]{2,1,0:T(4,128)S(1)}, f32[24,4,128]{2,1,0:T(4,128)S(1)}, f32[24,4,128]{2,1,0:T(4,128)S(1)}) custom-call(f32[32,128]{1,0:T(8,128)S(1)} %bitcast.35, f32[32,128]{1,0:T(8,128)S(1)} %bitcast.33, f32[32,128]{1,0:T(8,128)S(1)} %bitcast.31, f32[5120,128]{1,0:T(8,128)S(1)} %get-tuple-element.23.c_tail.c, ...), custom_call_target="tpu_custom_call" | custom-call | tf_op jit(solution)/shard_map/pallas_call | solution.py:365
  32.4 0.1 collective-permute-start.5
  32.5 4.6 %collective-permute-start.6 = (f32[24,4,128]{2,1,0:T(4,128)S(1)}, f32[24,4,128]{2,1,0:T(4,128)S(1)}, u32[]{:S(2)}, u32[]{:S(2)}) collective-permute-start(f32[24,4,128]{2,1,0:T(4,128)S(1)} %get-tuple-element.29), channel_id=1, source_target_pairs={{0,31},{1,2},{2,1},{3,4},{4,3},{5,6},{6,5},{7,8},{8,7},{9,10},{10,... | collective-permute-start | bytes 147464 | tf_op jit(solution)/shard_map/ppermute | solution.py:312
  37.1 0.0 collective-permute-done.5
  37.1 2.3 %collective-permute-done.6 = f32[24,4,128]{2,1,0:T(4,128)S(1)} collective-permute-done((f32[24,4,128]{2,1,0:T(4,128)S(1)}, f32[24,4,128]{2,1,0:T(4,128)S(1)}, u32[]{:S(2)}, u32[]{:S(2)}) %collective-permute-start.6) | collective-permute-done | bytes 49184 | tf_op jit(solution)/shard_map/ppermute | solution.py:312
  39.5 2.4 %collective-permute-start.9 = (f32[8,4,128]{2,1,0:T(4,128)S(1)}, f32[8,4,128]{2,1,0:T(4,128)S(1)}, u32[]{:S(2)}, u32[]{:S(2)}) collective-permute-start(f32[8,4,128]{2,1,0:T(4,128)S(1)} %get-tuple-element.35), channel_id=1, source_target_pairs={{0,96},{1,97},{2,98},{3,99},{4,100},{5,101},{6,102},{7,103},{8,104... | collective-permute-start | bytes 49160 | tf_op jit(solution)/shard_map/ppermute | solution.py:316
  41.9 2.3 %collective-permute-start.8 = (f32[8,4,128]{2,1,0:T(4,128)S(1)}, f32[8,4,128]{2,1,0:T(4,128)S(1)}, u32[]{:S(2)}, u32[]{:S(2)}) collective-permute-start(f32[8,4,128]{2,1,0:T(4,128)S(1)} %get-tuple-element.36), channel_id=1, source_target_pairs={{0,64},{1,65},{2,66},{3,67},{4,68},{5,69},{6,70},{7,71},{8,72},{9,... | collective-permute-start | bytes 49160 | tf_op jit(solution)/shard_map/ppermute | solution.py:316
  44.1 0.0 collective-permute-start.7
  44.1 0.5 %shard_map.67 = (f32[5120,128]{1,0:T(8,128)S(1)}, f32[5120,128]{1,0:T(8,128)S(1)}) custom-call(f32[5120,128]{1,0:T(8,128)S(1)} %get-tuple-element.23.c_tail.c, f32[5120,128]{1,0:T(8,128)S(1)} %get-tuple-element.24.d_tail.d), custom_call_target="tpu_custom_call" | custom-call | flops 2621440 | bytes 10485760 | tf_op jit(solution)/shard_map/pallas_call | solution.py:359
  44.6 1.3 %shard_map.68.u = f32[5120,128]{1,0:T(8,128)S(1)} custom-call(f32[32,128]{1,0:T(8,128)S(1)} %get-tuple-element.30.boundary, f32[5120,128]{1,0:T(8,128)S(1)} %get-tuple-element.31.y, f32[5120,128]{1,0:T(8,128)S(1)} %get-tuple-element.32.g, f32[5120,128]{1,0:T(8,128)S(1)} %get-tuple-element.33.w, f32[5120,128]{1,0:T(8,128)S(1)} %get-tuple-element.34.e, ...), custom_call_target="tpu_custom_call" | custom-call | flops 3932160 | bytes 23592960 | tf_op jit(solution)/shard_map/pallas_call | solution.py:377
  45.9 0.0 collective-permute-done.9
  46.0 1.2 %collective-permute-done.8 = f32[8,4,128]{2,1,0:T(4,128)S(1)} collective-permute-done((f32[8,4,128]{2,1,0:T(4,128)S(1)}, f32[8,4,128]{2,1,0:T(4,128)S(1)}, u32[]{:S(2)}, u32[]{:S(2)}) %collective-permute-start.8) | collective-permute-done | bytes 16416 | tf_op jit(solution)/shard_map/ppermute | solution.py:316
  47.1 2.0 %collective-permute-done.7 = f32[8,4,128]{2,1,0:T(4,128)S(1)} collective-permute-done((f32[8,4,128]{2,1,0:T(4,128)S(1)}, f32[8,4,128]{2,1,0:T(4,128)S(1)}, u32[]{:S(2)}, u32[]{:S(2)}) %collective-permute-start.7) | collective-permute-done | bytes 16416 | tf_op jit(solution)/shard_map/ppermute | solution.py:316
  49.1 1.6 %shard_map.69 = f32[5120,128]{1,0:T(8,128)} custom-call(f32[32,128]{1,0:T(8,128)S(1)} %bitcast.36, f32[32,128]{1,0:T(8,128)S(1)} %bitcast.34, f32[32,128]{1,0:T(8,128)S(1)} %bitcast.32, f32[5120,128]{1,0:T(8,128)S(1)} %shard_map.68.u, f32[5120,128]{1,0:T(8,128)S(1)} %get-tuple-element.32.g), custom_call_target="tpu_custom_call" | custom-call | flops 1310720 | bytes 7864320 | tf_op jit(solution)/shard_map/pallas_call | solution.py:389
  (4 shorter events, 0.0 us)
Async XLA Ops:
  0.0 20.3 %copy-start.5 = (s32[1,8,128]{2,1,0:T(8,128)S(1)}, s32[1,8,128]{2,1,0:T(8,128)}, u32[]{:S(2)}) copy-start(s32[1,8,128]{2,1,0:T(8,128)} %param.8) | copy-start | bytes 12292
  1.4 1.7 %copy-start = (f32[1,5120,128]{2,1,0:T(8,128)S(1)}, f32[1,5120,128]{2,1,0:T(8,128)}, u32[]{:S(2)}) copy-start(f32[1,5120,128]{2,1,0:T(8,128)} %param.6) | copy-start | bytes 7864324
  3.2 1.2 %copy-start.3 = (f32[1,2048,128]{2,1,0:T(8,128)S(1)}, f32[1,2048,128]{2,1,0:T(8,128)}, u32[]{:S(2)}) copy-start(f32[1,2048,128]{2,1,0:T(8,128)} %param.11) | copy-start | bytes 3145732
  4.4 0.7 %copy-start.4 = (s32[1,8,128]{2,1,0:T(8,128)S(1)}, s32[1,8,128]{2,1,0:T(8,128)}, u32[]{:S(2)}) copy-start(s32[1,8,128]{2,1,0:T(8,128)} %param.8) | copy-start | bytes 12292
  5.1 15.2 %copy-start.1 = (f32[1,5120,128]{2,1,0:T(8,128)S(1)}, f32[1,5120,128]{2,1,0:T(8,128)}, u32[]{:S(2)}) copy-start(f32[1,5120,128]{2,1,0:T(8,128)} %param.6) | copy-start | bytes 7864324
  7.1 6.5 %collective-permute-start = (f32[24,4,128]{2,1,0:T(4,128)S(1)}, f32[24,4,128]{2,1,0:T(4,128)S(1)}, u32[]{:S(2)}, u32[]{:S(2)}) collective-permute-start(f32[24,4,128]{2,1,0:T(4,128)S(1)} %get-tuple-element.21), channel_id=1, source_target_pairs={{0,1},{1,0},{2,3},{3,2},{4,5},{5,4},{6,7},{7,6},{8,9},{9,8},{10,11... | collective-permute-start | bytes 147464 | tf_op jit(solution)/shard_map/ppermute | solution.py:313
  7.2 8.2 %collective-permute-start.1 = (f32[24,4,128]{2,1,0:T(4,128)S(1)}, f32[24,4,128]{2,1,0:T(4,128)S(1)}, u32[]{:S(2)}, u32[]{:S(2)}) collective-permute-start(f32[24,4,128]{2,1,0:T(4,128)S(1)} %get-tuple-element.22), channel_id=1, source_target_pairs={{0,31},{1,2},{2,1},{3,4},{4,3},{5,6},{6,5},{7,8},{8,7},{9,10},{10,... | collective-permute-start | bytes 147464 | tf_op jit(solution)/shard_map/ppermute | solution.py:312
  15.4 15.1 %collective-permute-start.4 = (f32[8,4,128]{2,1,0:T(4,128)S(1)}, f32[8,4,128]{2,1,0:T(4,128)S(1)}, u32[]{:S(2)}, u32[]{:S(2)}) collective-permute-start(f32[8,4,128]{2,1,0:T(4,128)S(1)} %get-tuple-element.38), channel_id=1, source_target_pairs={{0,96},{1,97},{2,98},{3,99},{4,100},{5,101},{6,102},{7,103},{8,104... | collective-permute-start | bytes 49160 | tf_op jit(solution)/shard_map/ppermute | solution.py:316
  19.3 11.2 %collective-permute-start.3 = (f32[8,4,128]{2,1,0:T(4,128)S(1)}, f32[8,4,128]{2,1,0:T(4,128)S(1)}, u32[]{:S(2)}, u32[]{:S(2)}) collective-permute-start(f32[8,4,128]{2,1,0:T(4,128)S(1)} %get-tuple-element.39), channel_id=1, source_target_pairs={{0,64},{1,65},{2,66},{3,67},{4,68},{5,69},{6,70},{7,71},{8,72},{9,... | collective-permute-start | bytes 49160 | tf_op jit(solution)/shard_map/ppermute | solution.py:316
  19.3 11.2 %collective-permute-start.2 = (f32[8,4,128]{2,1,0:T(4,128)S(1)}, f32[8,4,128]{2,1,0:T(4,128)S(1)}, u32[]{:S(2)}, u32[]{:S(2)}) collective-permute-start(f32[8,4,128]{2,1,0:T(4,128)S(1)} %get-tuple-element.40), channel_id=1, source_target_pairs={{0,32},{1,33},{2,34},{3,35},{4,36},{5,37},{6,38},{7,39},{8,40},{9,... | collective-permute-start | bytes 49160 | tf_op jit(solution)/shard_map/ppermute | solution.py:316
  20.3 1.7 %copy-start.2 = (f32[1,5120,128]{2,1,0:T(8,128)S(1)}, f32[1,5120,128]{2,1,0:T(8,128)}, u32[]{:S(2)}) copy-start(f32[1,5120,128]{2,1,0:T(8,128)} %param.7) | copy-start | bytes 7864324
  32.4 4.7 %collective-permute-start.5 = (f32[24,4,128]{2,1,0:T(4,128)S(1)}, f32[24,4,128]{2,1,0:T(4,128)S(1)}, u32[]{:S(2)}, u32[]{:S(2)}) collective-permute-start(f32[24,4,128]{2,1,0:T(4,128)S(1)} %get-tuple-element.28), channel_id=1, source_target_pairs={{0,1},{1,0},{2,3},{3,2},{4,5},{5,4},{6,7},{7,6},{8,9},{9,8},{10,11... | collective-permute-start | bytes 147464 | tf_op jit(solution)/shard_map/ppermute | solution.py:313
  32.5 6.9 %collective-permute-start.6 = (f32[24,4,128]{2,1,0:T(4,128)S(1)}, f32[24,4,128]{2,1,0:T(4,128)S(1)}, u32[]{:S(2)}, u32[]{:S(2)}) collective-permute-start(f32[24,4,128]{2,1,0:T(4,128)S(1)} %get-tuple-element.29), channel_id=1, source_target_pairs={{0,31},{1,2},{2,1},{3,4},{4,3},{5,6},{6,5},{7,8},{8,7},{9,10},{10,... | collective-permute-start | bytes 147464 | tf_op jit(solution)/shard_map/ppermute | solution.py:312
  39.5 6.5 %collective-permute-start.9 = (f32[8,4,128]{2,1,0:T(4,128)S(1)}, f32[8,4,128]{2,1,0:T(4,128)S(1)}, u32[]{:S(2)}, u32[]{:S(2)}) collective-permute-start(f32[8,4,128]{2,1,0:T(4,128)S(1)} %get-tuple-element.35), channel_id=1, source_target_pairs={{0,96},{1,97},{2,98},{3,99},{4,100},{5,101},{6,102},{7,103},{8,104... | collective-permute-start | bytes 49160 | tf_op jit(solution)/shard_map/ppermute | solution.py:316
  41.9 5.2 %collective-permute-start.8 = (f32[8,4,128]{2,1,0:T(4,128)S(1)}, f32[8,4,128]{2,1,0:T(4,128)S(1)}, u32[]{:S(2)}, u32[]{:S(2)}) collective-permute-start(f32[8,4,128]{2,1,0:T(4,128)S(1)} %get-tuple-element.36), channel_id=1, source_target_pairs={{0,64},{1,65},{2,66},{3,67},{4,68},{5,69},{6,70},{7,71},{8,72},{9,... | collective-permute-start | bytes 49160 | tf_op jit(solution)/shard_map/ppermute | solution.py:316
  44.1 4.9 %collective-permute-start.7 = (f32[8,4,128]{2,1,0:T(4,128)S(1)}, f32[8,4,128]{2,1,0:T(4,128)S(1)}, u32[]{:S(2)}, u32[]{:S(2)}) collective-permute-start(f32[8,4,128]{2,1,0:T(4,128)S(1)} %get-tuple-element.37), channel_id=1, source_target_pairs={{0,32},{1,33},{2,34},{3,35},{4,36},{5,37},{6,38},{7,39},{8,40},{9,... | collective-permute-start | bytes 49160 | tf_op jit(solution)/shard_map/ppermute | solution.py:316

commit v2 on v1

v2 whole, which is shorter than its diff:
```python
from functools import partial

import jax
import jax.numpy as jnp
from jax import lax
from jax.experimental import pallas as pl
from jax.experimental.pallas import tpu as pltpu
from jax.sharding import PartitionSpec as P

CELLS = 128
LEV_ATM = 128
LEV_OCN = 80
TRC_ATM = 5
TRC_OCN = 8
COUPLED = 4
BLK = 8
WBLK = 16
PAIRS = WBLK // 2
ROWS = 5120
WIDE = BLK * COUPLED
CHUNK = 320
CHUNKS = ROWS // CHUNK
FETCH = 640
FETCHES = ROWS // FETCH
TAIL = 64
SECS = 4
ROTATIONS = SECS - 1
GOALS = 80

f32 = jnp.float32
bf16 = jnp.bfloat16
MIB = 1 << 20

ATM = (LEV_ATM, TRC_ATM)
OCN = (LEV_OCN, TRC_OCN)
AXES = ("sec", "col")


def call(kernel, outs, operands, in_hbm, scratch, limit, flops, nbytes, out_hbm=False, in_smem=0):
    vmem = pl.BlockSpec(memory_space=pltpu.VMEM)
    smem = pl.BlockSpec(memory_space=pltpu.SMEM)
    hbm = pl.BlockSpec(memory_space=pltpu.HBM)
    held = [pltpu.with_memory_space_constraint(x, pltpu.HBM) for x in operands[:in_hbm]]
    return pl.pallas_call(
        kernel,
        out_shape=[jax.ShapeDtypeStruct(shape, kind) for shape, kind in outs],
        in_specs=[hbm] * in_hbm + [vmem] * (len(operands) - in_hbm - in_smem) + [smem] * in_smem,
        out_specs=[hbm if out_hbm else vmem] * len(outs),
        scratch_shapes=scratch,
        compiler_params=pltpu.CompilerParams(vmem_limit_bytes=limit * MIB),
        cost_estimate=pl.CostEstimate(flops=flops, bytes_accessed=nbytes, transcendentals=0),
    )(*held, *operands[in_hbm:])


def per_component(body):
    ocean = lax.axis_index("sec") == SECS - 1
    pl.when(ocean)(partial(body, *OCN))
    pl.when(jnp.logical_not(ocean))(partial(body, *ATM))


def blocks_of(start, field, tracers):
    return pl.ds(start + field, BLK, stride=tracers)


def split(values):
    high = values.astype(bf16)
    return high, (values - high.astype(f32)).astype(bf16)


def doubled(surface):
    high, low = split(surface)
    return jnp.concatenate(
        [jnp.concatenate([high, high], axis=1), jnp.concatenate([low, low], axis=1)], axis=0
    )


def multiply(left, stacked, products, pair):
    both = jnp.dot(left, stacked, preferred_element_type=f32)
    both = both[:WIDE] + both[WIDE:]
    for half in range(2):
        for field in range(COUPLED):
            products[field, pl.ds((2 * pair + half) * BLK, BLK)] = both[
                field * BLK : (field + 1) * BLK, half * CELLS : (half + 1) * CELLS
            ]


def deliver(counts, products, targets):
    for first in range(0, COUPLED, 2):
        parts = [split(products[field]) for field in (first, first + 1)]
        right = jnp.concatenate(
            [jnp.concatenate([high, low], axis=0) for high, low in parts], axis=1
        )
        sums = jnp.dot(counts, right, preferred_element_type=f32)
        for t, target in enumerate(targets):
            for slot in range(ROTATIONS):
                row = (t * ROTATIONS + slot) * BLK
                for j in range(2):
                    target[slot * COUPLED + first + j] = sums[
                        row : row + BLK, j * CELLS : (j + 1) * CELLS
                    ]


def count_entries(listing, used):
    columns = lax.axis_size("col")
    sec = lax.axis_index("sec")
    col = lax.axis_index("col")
    source, goal, weight = listing[0], listing[1], listing[2]
    entries = goal.shape[1]
    device = lax.shift_right_logical(goal, BLK.bit_length() - 1)
    to_col = jnp.bitwise_and(device, columns - 1)
    to_sec = lax.shift_right_logical(device, columns.bit_length() - 1)
    slot = jnp.bitwise_and(to_sec - sec + (SECS - 1), SECS - 1)
    place = jnp.where(to_col == col, 0, jnp.where(to_col == jnp.bitwise_xor(col, 1), 1, 2))
    row = (place * ROTATIONS + slot) * BLK + jnp.bitwise_and(goal, BLK - 1)
    position = lax.broadcasted_iota(jnp.int32, (1, entries), 1)
    row = jnp.where(position < used, row, -1)
    combination = weight * BLK + jnp.bitwise_and(source, BLK - 1)
    goals = lax.broadcasted_iota(jnp.int32, (GOALS, entries), 0) == row
    combinations = lax.broadcasted_iota(jnp.int32, (WBLK * BLK, entries), 0) == combination
    counts = lax.dot_general(
        goals.astype(f32).astype(bf16),
        combinations.astype(f32).astype(bf16),
        (((1,), (1,)), ((), ())),
        preferred_element_type=f32,
    ).astype(bf16)
    return jnp.concatenate([counts, counts], axis=1)


def first_kernel(
    state, mask, listing, weights, count, own, near, far, stacked, counts, sea,
    tail, mask_buf, list_buf, w_buf, surface, products, sems, w_sems,
):
    small = [
        pltpu.make_async_copy(listing, list_buf, sems.at[0]),
        pltpu.make_async_copy(state.at[pl.ds(ROWS - TAIL, TAIL)], tail, sems.at[1]),
        pltpu.make_async_copy(mask, mask_buf, sems.at[2]),
    ]
    for copy in small:
        copy.start()

    def fetch(p):
        rows = pl.ds(p * 2 * CELLS, 2 * CELLS)
        return pltpu.make_async_copy(weights.at[rows], w_buf.at[rows], w_sems.at[p])

    for p in range(PAIRS):
        fetch(p).start()
    for copy in small:
        copy.wait()
    counts[...] = count_entries(list_buf[...], count[0, 0])
    cells = mask_buf[...].astype(f32)
    sea[...] = cells

    def component(levels, tracers):
        for field in range(COUPLED):
            surface[field * BLK : (field + 1) * BLK] = (
                tail[blocks_of(TAIL - BLK * tracers, field, tracers)] * cells
            )

    per_component(component)
    left = doubled(surface[...])
    for p in range(PAIRS):
        fetch(p).wait()
        base = p * 2 * CELLS
        high0, low0 = split(w_buf[base : base + CELLS])
        high1, low1 = split(w_buf[base + CELLS : base + 2 * CELLS])
        both = jnp.concatenate(
            [jnp.concatenate([high0, high1], axis=1), jnp.concatenate([low0, low1], axis=1)], axis=0
        )
        stacked[base : base + 2 * CELLS] = both
        multiply(left, both, products, p)
    deliver(counts[...], products, (own, near, far))


def middle_kernel(
    got1, got2, got3, y_top, g_top, sea, stacked, counts, boundary, own, near, far, surface, products
):
    for field in range(COUPLED):
        arrived = got1[field] + got2[field] + got3[field]
        boundary[field] = arrived
        surface[field * BLK : (field + 1) * BLK] = (
            y_top[field] + g_top[field] * arrived
        ) * sea[...]
    left = doubled(surface[...])
    for p in range(PAIRS):
        base = p * 2 * CELLS
        multiply(left, stacked[base : base + 2 * CELLS], products, p)
    deliver(counts[...], products, (own, near, far))


def sweep_kernel(state, mixing, sea, c, w, e, y, g, y_top, g_top, s_buf, r_buf, d, sems):
    def copies(i):
        rows = pl.ds(pl.multiple_of(i * FETCH, FETCH), FETCH)
        return (
            pltpu.make_async_copy(state.at[rows], s_buf.at[rows], sems.at[0, i]),
            pltpu.make_async_copy(mixing.at[rows], r_buf.at[rows], sems.at[1, i]),
        )

    for i in range(FETCHES):
        for copy in copies(i):
            copy.start()

    def component(levels, tracers):
        width = BLK * tracers
        zero = jnp.zeros((width, CELLS), f32)

        def eliminate(i, carry):
            @pl.when(lax.rem(i, FETCH // CHUNK) == 0)
            def _():
                for copy in copies(lax.div(i, FETCH // CHUNK)):
                    copy.wait()

            @pl.when(i == CHUNKS - 1)
            def _():
                for field in range(tracers):
                    r_buf[blocks_of(ROWS - width, field, tracers)] *= sea[...]

            r_above, c_above, d_above = carry
            for j in range(CHUNK // width):
                rows = pl.ds(pl.multiple_of(i * CHUNK + j * width, 8), width)
                r = r_buf[rows]
                inverse = 1.0 / (1.0 + r + r_above * (1.0 - c_above))
                lower = r_above * inverse
                c_above = r * inverse
                d_above = s_buf[rows] * inverse + lower * d_above
                w[rows] = inverse
                e[rows] = lower
                c[rows] = c_above
                d[rows] = d_above
                r_above = r
            return r_above, c_above, d_above

        lax.fori_loop(0, CHUNKS, eliminate, (zero, zero, zero))
        for field in range(COUPLED):
            rows = blocks_of(ROWS - width, field, tracers)
            y_top[field] = d[rows]
            g_top[field] = c[rows]

        def substitute(i, carry):
            y_below, g_below = carry
            for j in range(CHUNK // width):
                rows = pl.ds(pl.multiple_of(ROWS - i * CHUNK - (j + 1) * width, 8), width)
                upper = c[rows]
                y_below = d[rows] + upper * y_below
                g_below = upper * g_below
                y[rows] = y_below
                g[rows] = g_below
            return y_below, g_below

        lax.fori_loop(0, CHUNKS, substitute, (zero, jnp.ones_like(zero)))

    per_component(component)


def spread(values, tracers, wide):
    wide[...] = jnp.zeros_like(wide)
    for field in range(COUPLED):
        wide[blocks_of(0, field, tracers)] = values[field]


def again_kernel(boundary, y, g, w, e, c, u, wide):
    def component(levels, tracers):
        width = BLK * tracers
        spread(boundary, tracers, wide)
        zero = jnp.zeros((width, CELLS), f32)

        def down(i, above):
            b = wide[:width]
            for j in range(CHUNK // width):
                rows = pl.ds(pl.multiple_of(i * CHUNK + j * width, 8), width)
                above = (y[rows] + b * g[rows]) * w[rows] + e[rows] * above
                u[rows] = above
            return above

        def up(i, below):
            for j in range(CHUNK // width):
                rows = pl.ds(pl.multiple_of(ROWS - i * CHUNK - (j + 1) * width, 8), width)
                below = u[rows] + c[rows] * below
                u[rows] = below
            return below

        lax.fori_loop(0, CHUNKS, down, zero)
        lax.fori_loop(0, CHUNKS, up, zero)

    per_component(component)


def finish_kernel(got1, got2, got3, u, g, out, wide, buf, sems):
    arrived = [got1[field] + got2[field] + got3[field] for field in range(COUPLED)]

    def copy(i):
        rows = pl.ds(pl.multiple_of(i * CHUNK, CHUNK), CHUNK)
        return pltpu.make_async_copy(buf.at[rows], out.at[rows], sems.at[i])

    def component(levels, tracers):
        width = BLK * tracers
        spread(arrived, tracers, wide)

        def chunk(i, carry):
            b = wide[:width]
            for j in range(CHUNK // width):
                rows = pl.ds(pl.multiple_of(i * CHUNK + j * width, 8), width)
                buf[rows] = u[rows] + b * g[rows]
            copy(i).start()
            return carry

        lax.fori_loop(0, CHUNKS, chunk, 0)

    per_component(component)
    for i in range(CHUNKS):
        copy(i).wait()


def routes(secs, cols):
    every = [(s, c) for s in range(secs) for c in range(cols)]

    def table(move):
        result = []
        for s, c in every:
            to_s, to_c = move(s, c)
            result.append((s * cols + c, (to_s % secs) * cols + to_c % cols))
        return result

    near = table(lambda s, c: (s, c ^ 1))
    far = table(lambda s, c: (s, c + 1 if c % 2 else c - 1))
    turns = [table(lambda s, c, k=k: (s + k, c)) for k in range(1, secs)]
    return near, far, turns


def exchange(own, near, far, tables, work):
    to_near, to_far, turns = tables
    from_far = lax.ppermute(far, AXES, to_far)
    from_near = lax.ppermute(near, AXES, to_near)
    done = work()
    own, *done = lax.optimization_barrier((own, *done))
    total = own + from_near + from_far
    got = [
        lax.ppermute(total[k * COUPLED : (k + 1) * COUPLED], AXES, turns[k])
        for k in range(ROTATIONS)
    ]
    return got, done


def shards(column_state, mixing, surface_mask, pairings, pairing_count, remap_weights):
    tables = routes(lax.axis_size("sec"), lax.axis_size("col"))
    state = column_state[0]
    rates = mixing[0]
    listing = jnp.transpose(pairings, (2, 0, 1))
    points = ROWS * CELLS
    full = ((ROWS, CELLS), f32)
    payload = ((ROTATIONS * COUPLED, BLK, CELLS), f32)
    face = ((COUPLED, BLK, CELLS), f32)
    stack = ((PAIRS * 2 * CELLS, 2 * CELLS), bf16)
    table = ((GOALS, 2 * WBLK * BLK), bf16)
    surface = pltpu.VMEM((WIDE, CELLS), f32)
    products = pltpu.VMEM((COUPLED, WBLK * BLK, CELLS), f32)
    wide = pltpu.VMEM((TAIL, CELLS), f32)

    own, near, far, stacked, counts, sea = call(
        first_kernel,
        [payload, payload, payload, stack, table, ((BLK, CELLS), f32)],
        [state, surface_mask[0], listing, remap_weights[0], pairing_count],
        4,
        [
            pltpu.VMEM((TAIL, CELLS), f32),
            pltpu.VMEM((BLK, CELLS), jnp.int32),
            pltpu.VMEM(listing.shape, jnp.int32),
            pltpu.VMEM((WBLK * CELLS, CELLS), f32),
            surface,
            products,
            pltpu.SemaphoreType.DMA((3,)),
            pltpu.SemaphoreType.DMA((PAIRS,)),
        ],
        6,
        1 << 28,
        1 << 21,
        in_smem=1,
    )

    def sweeps():
        return call(
            sweep_kernel,
            [full] * 5 + [face] * 2,
            [state, rates, sea],
            2,
            [pltpu.VMEM(*full), pltpu.VMEM(*full), pltpu.VMEM(*full), pltpu.SemaphoreType.DMA((2, FETCHES))],
            10,
            20 * points,
            7 * points * 4,
        )

    got, (c, w, e, y, g, y_top, g_top) = exchange(own, near, far, tables, sweeps)

    boundary, own, near, far = call(
        middle_kernel,
        [face, payload, payload, payload],
        [*got, y_top, g_top, sea, stacked, counts],
        0,
        [surface, products],
        4,
        1 << 28,
        1 << 21,
    )

    def again():
        return call(
            again_kernel, [full], [boundary, y, g, w, e, c], 0, [wide], 2, 6 * points, 9 * points * 4
        )

    got, (u,) = exchange(own, near, far, tables, again)

    (out,) = call(
        finish_kernel,
        [full],
        [*got, u, g],
        0,
        [wide, pltpu.VMEM(*full), pltpu.SemaphoreType.DMA((CHUNKS,))],
        5,
        2 * points,
        3 * points * 4,
        True,
    )
    return out[None]


def solution(mesh):
    placed = (
        P("sec", "col", None),
        P("sec", "col", None),
        P("sec", "col", None),
        P("sec", "col", None),
        P("sec", "col"),
        P("sec", "col", None),
    )
    return jax.shard_map(
        shards, mesh=mesh, in_specs=placed, out_specs=P("sec", "col", None), check_vma=False
    )
```

time: 51.1 us -> 38.2 us (0.75)
  Pallas kernels: 15.8 us -> 9.55 us
  local copies, waits for them, and re-layouts: 6.19 us -> 0.01 us
  starting transfers between devices: 20.7 us -> 16.5 us
  waiting for transfers between devices: 7.21 us -> 11.3 us
    pallas_call x6 -> x5, Pallas kernels: 15.8 us -> 9.55 us  [call(): pl.pallas_call(kernel, out_shape=[jax.ShapeDtypeStruct(shape, kind) for s...]
    unnamed x13 -> x0, local copies, waits for them, and re-layouts: 6.18 us -> none
    ppermute x6, waiting for transfers between devices: 3.14 us -> 7.63 us  [exchange(): lax.ppermute(total[k * COUPLED:(k + 1) * COUPLED], AXES, turns[k])]
    ppermute x2, starting transfers between devices: 11 us -> 8.42 us  [exchange(): from_far = lax.ppermute(far, AXES, to_far)]
    ppermute x6, starting transfers between devices: 9.57 us -> 7.87 us  [exchange(): lax.ppermute(total[k * COUPLED:(k + 1) * COUPLED], AXES, turns[k])]
  transfers between devices with their start and end apart: 10 -> 10, of which waited for: 4 -> 6; matrix products, arithmetic and copies ran while one was open for 0% -> 0% of each run, Pallas kernels for 20% -> 12%
where the time goes in v2:
time: 38.2 us; the launch traced here: 38.1 us
  starting transfers between devices  16.5 us (43%)
  waiting for transfers between devices  11.3 us (30%)
  Pallas kernels  9.55 us (25%)
  between operations  0.75 us (2%)
    pallas_call x5, Pallas kernels, call(): pl.pallas_call(kernel, out_shape=[jax.ShapeDtypeStruct(shape, kind) for s...  9.55 us
    ppermute x2, starting transfers between devices, exchange(): from_far = lax.ppermute(far, AXES, to_far)  8.42 us
    ppermute x6, starting transfers between devices, exchange(): lax.ppermute(total[k * COUPLED:(k + 1) * COUPLED], AXES, turns[k])  7.87 us
    ppermute x6, waiting for transfers between devices, exchange(): lax.ppermute(total[k * COUPLED:(k + 1) * COUPLED], AXES, turns[k])  7.63 us
    ppermute x2, waiting for transfers between devices, exchange(): from_far = lax.ppermute(far, AXES, to_far)  3.65 us
  transfers between devices with their start and end apart: 10, of which 6 were waited for; matrix products, arithmetic and copies ran while one was open for 0% of the time, Pallas kernels for 12%

profile of v2, /device:TPU:0, one launch (start us, length us, event | category | flops | bytes accessed | tf_op | source)
XLA Modules:
  0.0 38.1 jit_solution(3961223198682420712)
XLA Ops:
  0.7 2.9 %shard_map.64 = (f32[12,8,128]{2,1,0:T(8,128)S(1)}, f32[12,8,128]{2,1,0:T(8,128)S(1)}, f32[12,8,128]{2,1,0:T(8,128)S(1)}, bf16[2048,256]{1,0:T(8,128)(2,1)S(1)},...) custom-call(f32[5120,128]{1,0:T(8,128)} %bitcast.6, s32[8,128]{1,0:T(8,128)} %bitcast.10, s32[3,1,54]{2,1,0:T(1,128)} %bitcast.11, ...), custom_call_target="tpu_custom_call" | custom-call | flops 268435456 | bytes 2097152 | tf_op jit(solution)/shard_map/pallas_call | solution.py:44
  3.6 0.1 collective-permute-start
  3.7 6.4 %collective-permute-start.1 = (f32[12,8,128]{2,1,0:T(8,128)S(1)}, f32[12,8,128]{2,1,0:T(8,128)S(1)}, u32[]{:S(2)}, u32[]{:S(2)}) collective-permute-start(f32[12,8,128]{2,1,0:T(8,128)S(1)} %get-tuple-element.43), channel_id=1, source_target_pairs={{0,31},{1,2},{2,1},{3,4},{4,3},{5,6},{6,5},{7,8},{8,7},{9,10},{10,... | collective-permute-start | bytes 147464 | tf_op jit(solution)/shard_map/ppermute | solution.py:331
  10.1 3.3 %shard_map.65 = (f32[5120,128]{1,0:T(8,128)S(1)}, f32[5120,128]{1,0:T(8,128)S(1)}, f32[5120,128]{1,0:T(8,128)S(1)}, f32[5120,128]{1,0:T(8,128)S(1)}, f32[5120,12...) custom-call(f32[5120,128]{1,0:T(8,128)} %bitcast.7, f32[5120,128]{1,0:T(8,128)} %bitcast.8, ...), custom_call_target="tpu_custom_call" | custom-call | flops 13107200 | bytes 18350080 | tf_op jit(solution)/shard_map/pallas_call | solution.py:44
  13.4 0.0 collective-permute-done
  13.4 0.0 collective-permute-done.1
  13.4 3.1 %collective-permute-start.4 = (f32[4,8,128]{2,1,0:T(8,128)S(1)}, f32[4,8,128]{2,1,0:T(8,128)S(1)}, u32[]{:S(2)}, u32[]{:S(2)}) collective-permute-start(f32[4,8,128]{2,1,0:T(8,128)S(1)} %get-tuple-element.62), channel_id=1, source_target_pairs={{0,96},{1,97},{2,98},{3,99},{4,100},{5,101},{6,102},{7,103},{8,104... | collective-permute-start | bytes 49160 | tf_op jit(solution)/shard_map/ppermute | solution.py:337
  16.5 0.6 %collective-permute-start.3 = (f32[4,8,128]{2,1,0:T(8,128)S(1)}, f32[4,8,128]{2,1,0:T(8,128)S(1)}, u32[]{:S(2)}, u32[]{:S(2)}) collective-permute-start(f32[4,8,128]{2,1,0:T(8,128)S(1)} %get-tuple-element.63), channel_id=1, source_target_pairs={{0,64},{1,65},{2,66},{3,67},{4,68},{5,69},{6,70},{7,71},{8,72},{9,... | collective-permute-start | bytes 49160 | tf_op jit(solution)/shard_map/ppermute | solution.py:337
  17.1 1.0 %collective-permute-start.2 = (f32[4,8,128]{2,1,0:T(8,128)S(1)}, f32[4,8,128]{2,1,0:T(8,128)S(1)}, u32[]{:S(2)}, u32[]{:S(2)}) collective-permute-start(f32[4,8,128]{2,1,0:T(8,128)S(1)} %get-tuple-element.64), channel_id=1, source_target_pairs={{0,32},{1,33},{2,34},{3,35},{4,36},{5,37},{6,38},{7,39},{8,40},{9,... | collective-permute-start | bytes 49160 | tf_op jit(solution)/shard_map/ppermute | solution.py:337
  18.1 0.0 collective-permute-done.4.got3
  18.1 3.6 %collective-permute-done.3.got2 = f32[4,8,128]{2,1,0:T(8,128)S(1)} collective-permute-done((f32[4,8,128]{2,1,0:T(8,128)S(1)}, f32[4,8,128]{2,1,0:T(8,128)S(1)}, u32[]{:S(2)}, u32[]{:S(2)}) %collective-permute-start.3) | collective-permute-done | bytes 16416 | tf_op jit(solution)/shard_map/ppermute | solution.py:337
  21.8 0.3 collective-permute-done.2.got1
  22.1 0.5 %shard_map.66 = (f32[4,8,128]{2,1,0:T(8,128)S(1)}, f32[12,8,128]{2,1,0:T(8,128)S(1)}, f32[12,8,128]{2,1,0:T(8,128)S(1)}, f32[12,8,128]{2,1,0:T(8,128)S(1)}) custom-call(f32[4,8,128]{2,1,0:T(8,128)S(1)} %collective-permute-done.2.got1, f32[4,8,128]{2,1,0:T(8,128)S(1)} %collective-permute-done.3.got2, f32[4,8,128]{2,1,0:T(8,128)S(1)} %collective-permute-done.4.got3, ...), custom_call_target="tpu_custom_call" | custom-call | flops 268435456 | bytes 2097152 | tf_op jit(solution)/shard_map/pallas_call | solution.py:44
  22.5 0.1 collective-permute-start.5
  22.6 2.0 %collective-permute-start.6 = (f32[12,8,128]{2,1,0:T(8,128)S(1)}, f32[12,8,128]{2,1,0:T(8,128)S(1)}, u32[]{:S(2)}, u32[]{:S(2)}) collective-permute-start(f32[12,8,128]{2,1,0:T(8,128)S(1)} %get-tuple-element.57), channel_id=1, source_target_pairs={{0,31},{1,2},{2,1},{3,4},{4,3},{5,6},{6,5},{7,8},{8,7},{9,10},{10,... | collective-permute-start | bytes 147464 | tf_op jit(solution)/shard_map/ppermute | solution.py:331
  24.6 1.3 %shard_map.67.u = f32[5120,128]{1,0:T(8,128)S(1)} custom-call(f32[4,8,128]{2,1,0:T(8,128)S(1)} %get-tuple-element.49.boundary, f32[5120,128]{1,0:T(8,128)S(1)} %get-tuple-element.50.y, f32[5120,128]{1,0:T(8,128)S(1)} %get-tuple-element.51.g, f32[5120,128]{1,0:T(8,128)S(1)} %get-tuple-element.52.w, f32[5120,128]{1,0:T(8,128)S(1)} %get-tuple-element.53.e, ...), custom_call_target="tpu_custom_call" | custom-call | flops 3932160 | bytes 23592960 | tf_op jit(solution)/shard_map/pallas_call | solution.py:44
  25.9 0.0 collective-permute-done.5
  25.9 3.6 %collective-permute-done.6 = f32[12,8,128]{2,1,0:T(8,128)S(1)} collective-permute-done((f32[12,8,128]{2,1,0:T(8,128)S(1)}, f32[12,8,128]{2,1,0:T(8,128)S(1)}, u32[]{:S(2)}, u32[]{:S(2)}) %collective-permute-start.6) | collective-permute-done | bytes 49184 | tf_op jit(solution)/shard_map/ppermute | solution.py:331
  29.6 0.5 %collective-permute-start.9 = (f32[4,8,128]{2,1,0:T(8,128)S(1)}, f32[4,8,128]{2,1,0:T(8,128)S(1)}, u32[]{:S(2)}, u32[]{:S(2)}) collective-permute-start(f32[4,8,128]{2,1,0:T(8,128)S(1)} %get-tuple-element.59), channel_id=1, source_target_pairs={{0,96},{1,97},{2,98},{3,99},{4,100},{5,101},{6,102},{7,103},{8,104... | collective-permute-start | bytes 49160 | tf_op jit(solution)/shard_map/ppermute | solution.py:337
  30.1 1.4 %collective-permute-start.8 = (f32[4,8,128]{2,1,0:T(8,128)S(1)}, f32[4,8,128]{2,1,0:T(8,128)S(1)}, u32[]{:S(2)}, u32[]{:S(2)}) collective-permute-start(f32[4,8,128]{2,1,0:T(8,128)S(1)} %get-tuple-element.60), channel_id=1, source_target_pairs={{0,64},{1,65},{2,66},{3,67},{4,68},{5,69},{6,70},{7,71},{8,72},{9,... | collective-permute-start | bytes 49160 | tf_op jit(solution)/shard_map/ppermute | solution.py:337
  31.5 1.3 %collective-permute-start.7 = (f32[4,8,128]{2,1,0:T(8,128)S(1)}, f32[4,8,128]{2,1,0:T(8,128)S(1)}, u32[]{:S(2)}, u32[]{:S(2)}) collective-permute-start(f32[4,8,128]{2,1,0:T(8,128)S(1)} %get-tuple-element.61), channel_id=1, source_target_pairs={{0,32},{1,33},{2,34},{3,35},{4,36},{5,37},{6,38},{7,39},{8,40},{9,... | collective-permute-start | bytes 49160 | tf_op jit(solution)/shard_map/ppermute | solution.py:337
  32.8 0.6 %collective-permute-done.9.got3 = f32[4,8,128]{2,1,0:T(8,128)S(1)} collective-permute-done((f32[4,8,128]{2,1,0:T(8,128)S(1)}, f32[4,8,128]{2,1,0:T(8,128)S(1)}, u32[]{:S(2)}, u32[]{:S(2)}) %collective-permute-start.9) | collective-permute-done | bytes 16416 | tf_op jit(solution)/shard_map/ppermute | solution.py:337
  33.4 1.9 %collective-permute-done.8.got2 = f32[4,8,128]{2,1,0:T(8,128)S(1)} collective-permute-done((f32[4,8,128]{2,1,0:T(8,128)S(1)}, f32[4,8,128]{2,1,0:T(8,128)S(1)}, u32[]{:S(2)}, u32[]{:S(2)}) %collective-permute-start.8) | collective-permute-done | bytes 16416 | tf_op jit(solution)/shard_map/ppermute | solution.py:337
  35.3 1.1 %collective-permute-done.7.got1 = f32[4,8,128]{2,1,0:T(8,128)S(1)} collective-permute-done((f32[4,8,128]{2,1,0:T(8,128)S(1)}, f32[4,8,128]{2,1,0:T(8,128)S(1)}, u32[]{:S(2)}, u32[]{:S(2)}) %collective-permute-start.7) | collective-permute-done | bytes 16416 | tf_op jit(solution)/shard_map/ppermute | solution.py:337
  36.4 1.7 %shard_map.68 = f32[5120,128]{1,0:T(8,128)} custom-call(f32[4,8,128]{2,1,0:T(8,128)S(1)} %collective-permute-done.7.got1, f32[4,8,128]{2,1,0:T(8,128)S(1)} %collective-permute-done.8.got2, f32[4,8,128]{2,1,0:T(8,128)S(1)} %collective-permute-done.9.got3, f32[5120,128]{1,0:T(8,128)S(1)} %shard_map.67.u, f32[5120,128]{1,0:T(8,128)S(1)} %get-tuple-element.51.g), custom_call_target="tpu_custom_call" | custom-call | flops 1310720 | bytes 7864320 | tf_op jit(solution)/shard_map/pallas_call | solution.py:44
  (4 shorter events, 0.0 us)
Async XLA Ops:
  3.6 9.8 %collective-permute-start = (f32[12,8,128]{2,1,0:T(8,128)S(1)}, f32[12,8,128]{2,1,0:T(8,128)S(1)}, u32[]{:S(2)}, u32[]{:S(2)}) collective-permute-start(f32[12,8,128]{2,1,0:T(8,128)S(1)} %get-tuple-element.42), channel_id=1, source_target_pairs={{0,1},{1,0},{2,3},{3,2},{4,5},{5,4},{6,7},{7,6},{8,9},{9,8},{10,11... | collective-permute-start | bytes 147464 | tf_op jit(solution)/shard_map/ppermute | solution.py:332
  3.7 9.7 %collective-permute-start.1 = (f32[12,8,128]{2,1,0:T(8,128)S(1)}, f32[12,8,128]{2,1,0:T(8,128)S(1)}, u32[]{:S(2)}, u32[]{:S(2)}) collective-permute-start(f32[12,8,128]{2,1,0:T(8,128)S(1)} %get-tuple-element.43), channel_id=1, source_target_pairs={{0,31},{1,2},{2,1},{3,4},{4,3},{5,6},{6,5},{7,8},{8,7},{9,10},{10,... | collective-permute-start | bytes 147464 | tf_op jit(solution)/shard_map/ppermute | solution.py:331
  13.4 4.7 %collective-permute-start.4 = (f32[4,8,128]{2,1,0:T(8,128)S(1)}, f32[4,8,128]{2,1,0:T(8,128)S(1)}, u32[]{:S(2)}, u32[]{:S(2)}) collective-permute-start(f32[4,8,128]{2,1,0:T(8,128)S(1)} %get-tuple-element.62), channel_id=1, source_target_pairs={{0,96},{1,97},{2,98},{3,99},{4,100},{5,101},{6,102},{7,103},{8,104... | collective-permute-start | bytes 49160 | tf_op jit(solution)/shard_map/ppermute | solution.py:337
  16.5 5.2 %collective-permute-start.3 = (f32[4,8,128]{2,1,0:T(8,128)S(1)}, f32[4,8,128]{2,1,0:T(8,128)S(1)}, u32[]{:S(2)}, u32[]{:S(2)}) collective-permute-start(f32[4,8,128]{2,1,0:T(8,128)S(1)} %get-tuple-element.63), channel_id=1, source_target_pairs={{0,64},{1,65},{2,66},{3,67},{4,68},{5,69},{6,70},{7,71},{8,72},{9,... | collective-permute-start | bytes 49160 | tf_op jit(solution)/shard_map/ppermute | solution.py:337
  17.1 4.9 %collective-permute-start.2 = (f32[4,8,128]{2,1,0:T(8,128)S(1)}, f32[4,8,128]{2,1,0:T(8,128)S(1)}, u32[]{:S(2)}, u32[]{:S(2)}) collective-permute-start(f32[4,8,128]{2,1,0:T(8,128)S(1)} %get-tuple-element.64), channel_id=1, source_target_pairs={{0,32},{1,33},{2,34},{3,35},{4,36},{5,37},{6,38},{7,39},{8,40},{9,... | collective-permute-start | bytes 49160 | tf_op jit(solution)/shard_map/ppermute | solution.py:337
  22.5 3.4 %collective-permute-start.5 = (f32[12,8,128]{2,1,0:T(8,128)S(1)}, f32[12,8,128]{2,1,0:T(8,128)S(1)}, u32[]{:S(2)}, u32[]{:S(2)}) collective-permute-start(f32[12,8,128]{2,1,0:T(8,128)S(1)} %get-tuple-element.56), channel_id=1, source_target_pairs={{0,1},{1,0},{2,3},{3,2},{4,5},{5,4},{6,7},{7,6},{8,9},{9,8},{10,11... | collective-permute-start | bytes 147464 | tf_op jit(solution)/shard_map/ppermute | solution.py:332
  22.6 6.9 %collective-permute-start.6 = (f32[12,8,128]{2,1,0:T(8,128)S(1)}, f32[12,8,128]{2,1,0:T(8,128)S(1)}, u32[]{:S(2)}, u32[]{:S(2)}) collective-permute-start(f32[12,8,128]{2,1,0:T(8,128)S(1)} %get-tuple-element.57), channel_id=1, source_target_pairs={{0,31},{1,2},{2,1},{3,4},{4,3},{5,6},{6,5},{7,8},{8,7},{9,10},{10,... | collective-permute-start | bytes 147464 | tf_op jit(solution)/shard_map/ppermute | solution.py:331
  29.6 3.8 %collective-permute-start.9 = (f32[4,8,128]{2,1,0:T(8,128)S(1)}, f32[4,8,128]{2,1,0:T(8,128)S(1)}, u32[]{:S(2)}, u32[]{:S(2)}) collective-permute-start(f32[4,8,128]{2,1,0:T(8,128)S(1)} %get-tuple-element.59), channel_id=1, source_target_pairs={{0,96},{1,97},{2,98},{3,99},{4,100},{5,101},{6,102},{7,103},{8,104... | collective-permute-start | bytes 49160 | tf_op jit(solution)/shard_map/ppermute | solution.py:337
  30.1 5.2 %collective-permute-start.8 = (f32[4,8,128]{2,1,0:T(8,128)S(1)}, f32[4,8,128]{2,1,0:T(8,128)S(1)}, u32[]{:S(2)}, u32[]{:S(2)}) collective-permute-start(f32[4,8,128]{2,1,0:T(8,128)S(1)} %get-tuple-element.60), channel_id=1, source_target_pairs={{0,64},{1,65},{2,66},{3,67},{4,68},{5,69},{6,70},{7,71},{8,72},{9,... | collective-permute-start | bytes 49160 | tf_op jit(solution)/shard_map/ppermute | solution.py:337
  31.5 4.9 %collective-permute-start.7 = (f32[4,8,128]{2,1,0:T(8,128)S(1)}, f32[4,8,128]{2,1,0:T(8,128)S(1)}, u32[]{:S(2)}, u32[]{:S(2)}) collective-permute-start(f32[4,8,128]{2,1,0:T(8,128)S(1)} %get-tuple-element.61), channel_id=1, source_target_pairs={{0,32},{1,33},{2,34},{3,35},{4,36},{5,37},{6,38},{7,39},{8,40},{9,... | collective-permute-start | bytes 49160 | tf_op jit(solution)/shard_map/ppermute | solution.py:337

commit v3 on v2

--- a/solution.py
+++ b/solution.py
@@ -20,8 +20,10 @@
 WIDE = BLK * COUPLED
 CHUNK = 320
 CHUNKS = ROWS // CHUNK
-FETCH = 640
-FETCHES = ROWS // FETCH
+LOADS = 4
+LOAD = ROWS // LOADS
+FETCHES = 2
+FETCH = WBLK * CELLS // FETCHES
 TAIL = 64
 SECS = 4
 ROTATIONS = SECS - 1
@@ -138,12 +140,12 @@
     for copy in small:
         copy.start()
 
-    def fetch(p):
-        rows = pl.ds(p * 2 * CELLS, 2 * CELLS)
-        return pltpu.make_async_copy(weights.at[rows], w_buf.at[rows], w_sems.at[p])
-
-    for p in range(PAIRS):
-        fetch(p).start()
+    def fetch(i):
+        rows = pl.ds(i * FETCH, FETCH)
+        return pltpu.make_async_copy(weights.at[rows], w_buf.at[rows], w_sems.at[i])
+
+    for i in range(FETCHES):
+        fetch(i).start()
     for copy in small:
         copy.wait()
     counts[...] = count_entries(list_buf[...], count[0, 0])
@@ -159,8 +161,9 @@
     per_component(component)
     left = doubled(surface[...])
     for p in range(PAIRS):
-        fetch(p).wait()
         base = p * 2 * CELLS
+        if base % FETCH == 0:
+            fetch(base // FETCH).wait()
         high0, low0 = split(w_buf[base : base + CELLS])
         high1, low1 = split(w_buf[base + CELLS : base + 2 * CELLS])
         both = jnp.concatenate(
@@ -172,13 +175,13 @@
 
 
 def middle_kernel(
-    got1, got2, got3, y_top, g_top, sea, stacked, counts, boundary, own, near, far, surface, products
+    got1, got2, got3, d_top, c_top, sea, stacked, counts, boundary, own, near, far, surface, products
 ):
     for field in range(COUPLED):
         arrived = got1[field] + got2[field] + got3[field]
         boundary[field] = arrived
         surface[field * BLK : (field + 1) * BLK] = (
-            y_top[field] + g_top[field] * arrived
+            d_top[field] + c_top[field] * arrived
         ) * sea[...]
     left = doubled(surface[...])
     for p in range(PAIRS):
@@ -187,15 +190,21 @@
     deliver(counts[...], products, (own, near, far))
 
 
-def sweep_kernel(state, mixing, sea, c, w, e, y, g, y_top, g_top, s_buf, r_buf, d, sems):
+def spread(values, tracers, wide):
+    wide[...] = jnp.zeros_like(wide)
+    for field in range(COUPLED):
+        wide[blocks_of(0, field, tracers)] = values[field]
+
+
+def eliminate_kernel(state, mixing, sea, c, w, e, d, c_top, d_top, s_buf, r_buf, sems):
     def copies(i):
-        rows = pl.ds(pl.multiple_of(i * FETCH, FETCH), FETCH)
+        rows = pl.ds(pl.multiple_of(i * LOAD, LOAD), LOAD)
         return (
-            pltpu.make_async_copy(state.at[rows], s_buf.at[rows], sems.at[0, i]),
-            pltpu.make_async_copy(mixing.at[rows], r_buf.at[rows], sems.at[1, i]),
+            pltpu.make_async_copy(mixing.at[rows], r_buf.at[rows], sems.at[0, i]),
+            pltpu.make_async_copy(state.at[rows], s_buf.at[rows], sems.at[1, i]),
         )
 
-    for i in range(FETCHES):
+    for i in range(LOADS):
         for copy in copies(i):
             copy.start()
 
@@ -203,10 +212,10 @@
         width = BLK * tracers
         zero = jnp.zeros((width, CELLS), f32)
 
-        def eliminate(i, carry):
-            @pl.when(lax.rem(i, FETCH // CHUNK) == 0)
+        def chunk(i, carry):
+            @pl.when(lax.rem(i, LOAD // CHUNK) == 0)
             def _():
-                for copy in copies(lax.div(i, FETCH // CHUNK)):
+                for copy in copies(lax.div(i, LOAD // CHUNK)):
                     copy.wait()
 
             @pl.when(i == CHUNKS - 1)
@@ -229,55 +238,51 @@
                 r_above = r
             return r_above, c_above, d_above
 
-        lax.fori_loop(0, CHUNKS, eliminate, (zero, zero, zero))
+        lax.fori_loop(0, CHUNKS, chunk, (zero, zero, zero))
         for field in range(COUPLED):
             rows = blocks_of(ROWS - width, field, tracers)
-            y_top[field] = d[rows]
-            g_top[field] = c[rows]
-
-        def substitute(i, carry):
-            y_below, g_below = carry
-            for j in range(CHUNK // width):
-                rows = pl.ds(pl.multiple_of(ROWS - i * CHUNK - (j + 1) * width, 8), width)
-                upper = c[rows]
-                y_below = d[rows] + upper * y_below
-                g_below = upper * g_below
-                y[rows] = y_below
-                g[rows] = g_below
-            return y_below, g_below
-
-        lax.fori_loop(0, CHUNKS, substitute, (zero, jnp.ones_like(zero)))
+            c_top[field] = c[rows]
+            d_top[field] = d[rows]
 
     per_component(component)
 
 
-def spread(values, tracers, wide):
-    wide[...] = jnp.zeros_like(wide)
-    for field in range(COUPLED):
-        wide[blocks_of(0, field, tracers)] = values[field]
-
-
-def again_kernel(boundary, y, g, w, e, c, u, wide):
+def again_kernel(boundary, c, w, e, d, u, g, wide):
     def component(levels, tracers):
         width = BLK * tracers
+        per_chunk = CHUNK // width
         spread(boundary, tracers, wide)
         zero = jnp.zeros((width, CELLS), f32)
 
+        def from_end(i, j):
+            return pl.ds(pl.multiple_of(ROWS - i * CHUNK - (j + 1) * width, 8), width)
+
+        def first(i, carry):
+            x_below, g_below = carry
+            for j in range(per_chunk):
+                rows = from_end(i, j)
+                upper = c[rows]
+                x_below = d[rows] + upper * x_below
+                g_below = upper * g_below
+                u[rows] = x_below
+                g[rows] = g_below
+            return x_below, g_below
+
         def down(i, above):
-            b = wide[:width]
-            for j in range(CHUNK // width):
+            for j in range(per_chunk):
                 rows = pl.ds(pl.multiple_of(i * CHUNK + j * width, 8), width)
-                above = (y[rows] + b * g[rows]) * w[rows] + e[rows] * above
+                above = u[rows] * w[rows] + e[rows] * above
                 u[rows] = above
             return above
 
         def up(i, below):
-            for j in range(CHUNK // width):
-                rows = pl.ds(pl.multiple_of(ROWS - i * CHUNK - (j + 1) * width, 8), width)
+            for j in range(per_chunk):
+                rows = from_end(i, j)
                 below = u[rows] + c[rows] * below
                 u[rows] = below
             return below
 
+        lax.fori_loop(0, CHUNKS, first, (wide[:width], jnp.ones_like(zero)))
         lax.fori_loop(0, CHUNKS, down, zero)
         lax.fori_loop(0, CHUNKS, up, zero)
 
@@ -326,18 +331,20 @@
     return near, far, turns
 
 
-def exchange(own, near, far, tables, work):
-    to_near, to_far, turns = tables
-    from_far = lax.ppermute(far, AXES, to_far)
-    from_near = lax.ppermute(near, AXES, to_near)
-    done = work()
-    own, *done = lax.optimization_barrier((own, *done))
+def along_col(own, near, far, tables):
+    from_near = lax.ppermute(near, AXES, tables[0])
+    from_far = lax.ppermute(far, AXES, tables[1])
+    return own, from_near, from_far
+
+
+def along_sec(parts, tables):
+    own, from_near, from_far = parts
     total = own + from_near + from_far
     got = [
-        lax.ppermute(total[k * COUPLED : (k + 1) * COUPLED], AXES, turns[k])
+        lax.ppermute(total[k * COUPLED : (k + 1) * COUPLED], AXES, tables[2][k])
         for k in range(ROTATIONS)
     ]
-    return got, done
+    return total, got
 
 
 def shards(column_state, mixing, surface_mask, pairings, pairing_count, remap_weights):
@@ -368,7 +375,7 @@
             surface,
             products,
             pltpu.SemaphoreType.DMA((3,)),
-            pltpu.SemaphoreType.DMA((PAIRS,)),
+            pltpu.SemaphoreType.DMA((FETCHES,)),
         ],
         6,
         1 << 28,
@@ -376,24 +383,23 @@
         in_smem=1,
     )
 
-    def sweeps():
-        return call(
-            sweep_kernel,
-            [full] * 5 + [face] * 2,
-            [state, rates, sea],
-            2,
-            [pltpu.VMEM(*full), pltpu.VMEM(*full), pltpu.VMEM(*full), pltpu.SemaphoreType.DMA((2, FETCHES))],
-            10,
-            20 * points,
-            7 * points * 4,
-        )
-
-    got, (c, w, e, y, g, y_top, g_top) = exchange(own, near, far, tables, sweeps)
-
+    parts = along_col(own, near, far, tables)
+    total, got = along_sec(parts, tables)
+    total, sea = lax.optimization_barrier((total, sea))
+    c, w, e, d, c_top, d_top = call(
+        eliminate_kernel,
+        [full] * 4 + [face] * 2,
+        [state, rates, sea],
+        2,
+        [pltpu.VMEM(*full), pltpu.VMEM(*full), pltpu.SemaphoreType.DMA((2, LOADS))],
+        7,
+        20 * points,
+        6 * points * 4,
+    )
     boundary, own, near, far = call(
         middle_kernel,
         [face, payload, payload, payload],
-        [*got, y_top, g_top, sea, stacked, counts],
+        [*got, d_top, c_top, sea, stacked, counts],
         0,
         [surface, products],
         4,
@@ -401,12 +407,12 @@
         1 << 21,
     )
 
-    def again():
-        return call(
-            again_kernel, [full], [boundary, y, g, w, e, c], 0, [wide], 2, 6 * points, 9 * points * 4
-        )
-
-    got, (u,) = exchange(own, near, far, tables, again)
+    parts = along_col(own, near, far, tables)
+    u, g = call(
+        again_kernel, [full] * 2, [boundary, c, w, e, d], 0, [wide], 2, 9 * points, 12 * points * 4
+    )
+    parts, u, g = lax.optimization_barrier((parts, u, g))
+    _, got = along_sec(parts, tables)
 
     (out,) = call(
         finish_kernel,

time: 38.2 us -> 35.5 us (0.929)
  waiting for transfers between devices: 11.3 us -> 6.42 us
  starting transfers between devices: 16.5 us -> 19.8 us
  Pallas kernels: 9.55 us -> 8.42 us
    ppermute x10, waiting for transfers between devices: 11.3 us -> 6.42 us  [the longest x6 3.64 us: along_sec(): lax.ppermute(total[k * COUPLED:(k + 1) * COUPLED], AXES, tables[2][k])]
    ppermute x10, starting transfers between devices: 16.5 us -> 19.8 us  [the longest x2 10.1 us: along_col(): from_far = lax.ppermute(far, AXES, tables[1])]
    pallas_call x5, Pallas kernels: 9.55 us -> 8.42 us  [call(): pl.pallas_call(kernel, out_shape=[jax.ShapeDtypeStruct(shape, kind) for s...]
  transfers between devices with their start and end apart: 10 -> 10, of which waited for: 6 -> 5; matrix products, arithmetic and copies ran while one was open for 0% -> 0% of each run, Pallas kernels for 12% -> 13%
where the time goes in v3:
time: 35.5 us; the launch traced here: 35.4 us
  starting transfers between devices  19.8 us (56%)
  Pallas kernels  8.42 us (24%)
  waiting for transfers between devices  6.42 us (18%)
  between operations  0.75 us (2%)
    ppermute x2, starting transfers between devices, along_col(): from_far = lax.ppermute(far, AXES, tables[1])  10.1 us
    ppermute x6, starting transfers between devices, along_sec(): lax.ppermute(total[k * COUPLED:(k + 1) * COUPLED], AXES, tables[2][k])  9.54 us
    pallas_call x5, Pallas kernels, call(): pl.pallas_call(kernel, out_shape=[jax.ShapeDtypeStruct(shape, kind) for s...  8.42 us
    ppermute x6, waiting for transfers between devices, along_sec(): lax.ppermute(total[k * COUPLED:(k + 1) * COUPLED], AXES, tables[2][k])  3.64 us
    ppermute x2, waiting for transfers between devices, along_col(): from_far = lax.ppermute(far, AXES, tables[1])  2.77 us
  transfers between devices with their start and end apart: 10, of which 5 were waited for; matrix products, arithmetic and copies ran while one was open for 0% of the time, Pallas kernels for 13%

profile of v3, /device:TPU:0, one launch (start us, length us, event | category | flops | bytes accessed | tf_op | source)
XLA Modules:
  0.0 35.4 jit_solution(17168391688358719298)
XLA Ops:
  0.7 1.8 %shard_map.64 = (f32[12,8,128]{2,1,0:T(8,128)S(1)}, f32[12,8,128]{2,1,0:T(8,128)S(1)}, f32[12,8,128]{2,1,0:T(8,128)S(1)}, bf16[2048,256]{1,0:T(8,128)(2,1)S(1)},...) custom-call(f32[5120,128]{1,0:T(8,128)} %bitcast.6, s32[8,128]{1,0:T(8,128)} %bitcast.10, s32[3,1,54]{2,1,0:T(1,128)} %bitcast.11, ...), custom_call_target="tpu_custom_call" | custom-call | flops 268435456 | bytes 2097152 | tf_op jit(solution)/shard_map/pallas_call | solution.py:46
  2.5 5.8 %collective-permute-start.1 = (f32[12,8,128]{2,1,0:T(8,128)S(1)}, f32[12,8,128]{2,1,0:T(8,128)S(1)}, u32[]{:S(2)}, u32[]{:S(2)}) collective-permute-start(f32[12,8,128]{2,1,0:T(8,128)S(1)} %get-tuple-element.31), channel_id=1, source_target_pairs={{0,31},{1,2},{2,1},{3,4},{4,3},{5,6},{6,5},{7,8},{8,7},{9,10},{10,... | collective-permute-start | bytes 147464 | tf_op jit(solution)/shard_map/ppermute | solution.py:336
  8.3 0.0 collective-permute-start
  8.3 1.8 %collective-permute-done.1 = f32[12,8,128]{2,1,0:T(8,128)S(1)} collective-permute-done((f32[12,8,128]{2,1,0:T(8,128)S(1)}, f32[12,8,128]{2,1,0:T(8,128)S(1)}, u32[]{:S(2)}, u32[]{:S(2)}) %collective-permute-start.1) | collective-permute-done | bytes 49184 | tf_op jit(solution)/shard_map/ppermute | solution.py:336
  10.1 0.0 collective-permute-done
  10.1 1.6 %collective-permute-start.2 = (f32[4,8,128]{2,1,0:T(8,128)S(1)}, f32[4,8,128]{2,1,0:T(8,128)S(1)}, u32[]{:S(2)}, u32[]{:S(2)}) collective-permute-start(f32[4,8,128]{2,1,0:T(8,128)S(1)} %get-tuple-element.58), channel_id=1, source_target_pairs={{0,32},{1,33},{2,34},{3,35},{4,36},{5,37},{6,38},{7,39},{8,40},{9,... | collective-permute-start | bytes 49160 | tf_op jit(solution)/shard_map/ppermute | solution.py:344
  11.8 2.9 %collective-permute-start.3 = (f32[4,8,128]{2,1,0:T(8,128)S(1)}, f32[4,8,128]{2,1,0:T(8,128)S(1)}, u32[]{:S(2)}, u32[]{:S(2)}) collective-permute-start(f32[4,8,128]{2,1,0:T(8,128)S(1)} %get-tuple-element.57), channel_id=1, source_target_pairs={{0,64},{1,65},{2,66},{3,67},{4,68},{5,69},{6,70},{7,71},{8,72},{9,... | collective-permute-start | bytes 49160 | tf_op jit(solution)/shard_map/ppermute | solution.py:344
  14.7 1.4 %collective-permute-start.4 = (f32[4,8,128]{2,1,0:T(8,128)S(1)}, f32[4,8,128]{2,1,0:T(8,128)S(1)}, u32[]{:S(2)}, u32[]{:S(2)}) collective-permute-start(f32[4,8,128]{2,1,0:T(8,128)S(1)} %get-tuple-element.56), channel_id=1, source_target_pairs={{0,96},{1,97},{2,98},{3,99},{4,100},{5,101},{6,102},{7,103},{8,104... | collective-permute-start | bytes 49160 | tf_op jit(solution)/shard_map/ppermute | solution.py:344
  16.0 2.9 %shard_map.65 = (f32[5120,128]{1,0:T(8,128)S(1)}, f32[5120,128]{1,0:T(8,128)S(1)}, f32[5120,128]{1,0:T(8,128)S(1)}, f32[5120,128]{1,0:T(8,128)S(1)}, f32[4,8,128]{2,1,0:T(8,128)S(1)}, /*index=5*/f32[4,8,128]{2,1,0:T(8,128)S(1)}) custom-call(f32[5120,128]{1,0:T(8,128)} %bitcast.7, f32[5120,128]{1,0:T(8,128)} %bitcast.8, f32[8,128]{1,0:T(8,128)S(1)} %get-tuple-element.33.sea), custom_call_target="tpu_custom_call" | custom-call | flops 13107200 | bytes 15728640 | tf_op jit(solution)/shard_map/pallas_call | solution.py:46
  18.9 0.0 collective-permute-done.2.got1
  18.9 0.0 collective-permute-done.3.got2
  19.0 0.0 collective-permute-done.4.got3
  19.0 0.5 %shard_map.66 = (f32[4,8,128]{2,1,0:T(8,128)S(1)}, f32[12,8,128]{2,1,0:T(8,128)S(1)}, f32[12,8,128]{2,1,0:T(8,128)S(1)}, f32[12,8,128]{2,1,0:T(8,128)S(1)}) custom-call(f32[4,8,128]{2,1,0:T(8,128)S(1)} %collective-permute-done.2.got1, f32[4,8,128]{2,1,0:T(8,128)S(1)} %collective-permute-done.3.got2, f32[4,8,128]{2,1,0:T(8,128)S(1)} %collective-permute-done.4.got3, ...), custom_call_target="tpu_custom_call" | custom-call | flops 268435456 | bytes 2097152 | tf_op jit(solution)/shard_map/pallas_call | solution.py:46
  19.4 0.1 collective-permute-start.5
  19.5 4.3 %collective-permute-start.6 = (f32[12,8,128]{2,1,0:T(8,128)S(1)}, f32[12,8,128]{2,1,0:T(8,128)S(1)}, u32[]{:S(2)}, u32[]{:S(2)}) collective-permute-start(f32[12,8,128]{2,1,0:T(8,128)S(1)} %get-tuple-element.40), channel_id=1, source_target_pairs={{0,31},{1,2},{2,1},{3,4},{4,3},{5,6},{6,5},{7,8},{8,7},{9,10},{10,... | collective-permute-start | bytes 147464 | tf_op jit(solution)/shard_map/ppermute | solution.py:336
  23.8 1.6 %shard_map.67 = (f32[5120,128]{1,0:T(8,128)S(1)}, f32[5120,128]{1,0:T(8,128)S(1)}) custom-call(f32[4,8,128]{2,1,0:T(8,128)S(1)} %get-tuple-element.41.boundary, f32[5120,128]{1,0:T(8,128)S(1)} %get-tuple-element.42.c, f32[5120,128]{1,0:T(8,128)S(1)} %get-tuple-element.43.w, f32[5120,128]{1,0:T(8,128)S(1)} %get-tuple-element.44.e, ...), custom_call_target="tpu_custom_call" | custom-call | flops 5898240 | bytes 31457280 | tf_op jit(solution)/shard_map/pallas_call | solution.py:46
  25.4 0.0 collective-permute-done.5
  25.4 1.0 %collective-permute-done.6 = f32[12,8,128]{2,1,0:T(8,128)S(1)} collective-permute-done((f32[12,8,128]{2,1,0:T(8,128)S(1)}, f32[12,8,128]{2,1,0:T(8,128)S(1)}, u32[]{:S(2)}, u32[]{:S(2)}) %collective-permute-start.6) | collective-permute-done | bytes 49184 | tf_op jit(solution)/shard_map/ppermute | solution.py:336
  26.5 0.7 %collective-permute-start.7 = (f32[4,8,128]{2,1,0:T(8,128)S(1)}, f32[4,8,128]{2,1,0:T(8,128)S(1)}, u32[]{:S(2)}, u32[]{:S(2)}) collective-permute-start(f32[4,8,128]{2,1,0:T(8,128)S(1)} %get-tuple-element.55), channel_id=1, source_target_pairs={{0,32},{1,33},{2,34},{3,35},{4,36},{5,37},{6,38},{7,39},{8,40},{9,... | collective-permute-start | bytes 49160 | tf_op jit(solution)/shard_map/ppermute | solution.py:344
  27.2 2.8 %collective-permute-start.8 = (f32[4,8,128]{2,1,0:T(8,128)S(1)}, f32[4,8,128]{2,1,0:T(8,128)S(1)}, u32[]{:S(2)}, u32[]{:S(2)}) collective-permute-start(f32[4,8,128]{2,1,0:T(8,128)S(1)} %get-tuple-element.54), channel_id=1, source_target_pairs={{0,64},{1,65},{2,66},{3,67},{4,68},{5,69},{6,70},{7,71},{8,72},{9,... | collective-permute-start | bytes 49160 | tf_op jit(solution)/shard_map/ppermute | solution.py:344
  30.0 0.1 collective-permute-start.9
  30.1 1.4 %collective-permute-done.7.got1 = f32[4,8,128]{2,1,0:T(8,128)S(1)} collective-permute-done((f32[4,8,128]{2,1,0:T(8,128)S(1)}, f32[4,8,128]{2,1,0:T(8,128)S(1)}, u32[]{:S(2)}, u32[]{:S(2)}) %collective-permute-start.7) | collective-permute-done | bytes 16416 | tf_op jit(solution)/shard_map/ppermute | solution.py:344
  31.5 1.0 %collective-permute-done.8.got2 = f32[4,8,128]{2,1,0:T(8,128)S(1)} collective-permute-done((f32[4,8,128]{2,1,0:T(8,128)S(1)}, f32[4,8,128]{2,1,0:T(8,128)S(1)}, u32[]{:S(2)}, u32[]{:S(2)}) %collective-permute-start.8) | collective-permute-done | bytes 16416 | tf_op jit(solution)/shard_map/ppermute | solution.py:344
  32.4 1.3 %collective-permute-done.9.got3 = f32[4,8,128]{2,1,0:T(8,128)S(1)} collective-permute-done((f32[4,8,128]{2,1,0:T(8,128)S(1)}, f32[4,8,128]{2,1,0:T(8,128)S(1)}, u32[]{:S(2)}, u32[]{:S(2)}) %collective-permute-start.9) | collective-permute-done | bytes 16416 | tf_op jit(solution)/shard_map/ppermute | solution.py:344
  33.7 1.6 %shard_map.68 = f32[5120,128]{1,0:T(8,128)} custom-call(f32[4,8,128]{2,1,0:T(8,128)S(1)} %collective-permute-done.7.got1, f32[4,8,128]{2,1,0:T(8,128)S(1)} %collective-permute-done.8.got2, f32[4,8,128]{2,1,0:T(8,128)S(1)} %collective-permute-done.9.got3, f32[5120,128]{1,0:T(8,128)S(1)} %get-tuple-element.51.u, f32[5120,128]{1,0:T(8,128)S(1)} %get-tuple-element.52.g), custom_call_target="tpu_custom_call" | custom-call | flops 1310720 | bytes 7864320 | tf_op jit(solution)/shard_map/pallas_call | solution.py:46
  (4 shorter events, 0.0 us)
Async XLA Ops:
  2.5 7.6 %collective-permute-start.1 = (f32[12,8,128]{2,1,0:T(8,128)S(1)}, f32[12,8,128]{2,1,0:T(8,128)S(1)}, u32[]{:S(2)}, u32[]{:S(2)}) collective-permute-start(f32[12,8,128]{2,1,0:T(8,128)S(1)} %get-tuple-element.31), channel_id=1, source_target_pairs={{0,31},{1,2},{2,1},{3,4},{4,3},{5,6},{6,5},{7,8},{8,7},{9,10},{10,... | collective-permute-start | bytes 147464 | tf_op jit(solution)/shard_map/ppermute | solution.py:336
  8.3 1.8 %collective-permute-start = (f32[12,8,128]{2,1,0:T(8,128)S(1)}, f32[12,8,128]{2,1,0:T(8,128)S(1)}, u32[]{:S(2)}, u32[]{:S(2)}) collective-permute-start(f32[12,8,128]{2,1,0:T(8,128)S(1)} %get-tuple-element.30), channel_id=1, source_target_pairs={{0,1},{1,0},{2,3},{3,2},{4,5},{5,4},{6,7},{7,6},{8,9},{9,8},{10,11... | collective-permute-start | bytes 147464 | tf_op jit(solution)/shard_map/ppermute | solution.py:335
  10.1 8.8 %collective-permute-start.2 = (f32[4,8,128]{2,1,0:T(8,128)S(1)}, f32[4,8,128]{2,1,0:T(8,128)S(1)}, u32[]{:S(2)}, u32[]{:S(2)}) collective-permute-start(f32[4,8,128]{2,1,0:T(8,128)S(1)} %get-tuple-element.58), channel_id=1, source_target_pairs={{0,32},{1,33},{2,34},{3,35},{4,36},{5,37},{6,38},{7,39},{8,40},{9,... | collective-permute-start | bytes 49160 | tf_op jit(solution)/shard_map/ppermute | solution.py:344
  11.8 7.2 %collective-permute-start.3 = (f32[4,8,128]{2,1,0:T(8,128)S(1)}, f32[4,8,128]{2,1,0:T(8,128)S(1)}, u32[]{:S(2)}, u32[]{:S(2)}) collective-permute-start(f32[4,8,128]{2,1,0:T(8,128)S(1)} %get-tuple-element.57), channel_id=1, source_target_pairs={{0,64},{1,65},{2,66},{3,67},{4,68},{5,69},{6,70},{7,71},{8,72},{9,... | collective-permute-start | bytes 49160 | tf_op jit(solution)/shard_map/ppermute | solution.py:344
  14.7 4.3 %collective-permute-start.4 = (f32[4,8,128]{2,1,0:T(8,128)S(1)}, f32[4,8,128]{2,1,0:T(8,128)S(1)}, u32[]{:S(2)}, u32[]{:S(2)}) collective-permute-start(f32[4,8,128]{2,1,0:T(8,128)S(1)} %get-tuple-element.56), channel_id=1, source_target_pairs={{0,96},{1,97},{2,98},{3,99},{4,100},{5,101},{6,102},{7,103},{8,104... | collective-permute-start | bytes 49160 | tf_op jit(solution)/shard_map/ppermute | solution.py:344
  19.4 6.0 %collective-permute-start.5 = (f32[12,8,128]{2,1,0:T(8,128)S(1)}, f32[12,8,128]{2,1,0:T(8,128)S(1)}, u32[]{:S(2)}, u32[]{:S(2)}) collective-permute-start(f32[12,8,128]{2,1,0:T(8,128)S(1)} %get-tuple-element.39), channel_id=1, source_target_pairs={{0,1},{1,0},{2,3},{3,2},{4,5},{5,4},{6,7},{7,6},{8,9},{9,8},{10,11... | collective-permute-start | bytes 147464 | tf_op jit(solution)/shard_map/ppermute | solution.py:335
  19.5 6.9 %collective-permute-start.6 = (f32[12,8,128]{2,1,0:T(8,128)S(1)}, f32[12,8,128]{2,1,0:T(8,128)S(1)}, u32[]{:S(2)}, u32[]{:S(2)}) collective-permute-start(f32[12,8,128]{2,1,0:T(8,128)S(1)} %get-tuple-element.40), channel_id=1, source_target_pairs={{0,31},{1,2},{2,1},{3,4},{4,3},{5,6},{6,5},{7,8},{8,7},{9,10},{10,... | collective-permute-start | bytes 147464 | tf_op jit(solution)/shard_map/ppermute | solution.py:336
  26.5 5.0 %collective-permute-start.7 = (f32[4,8,128]{2,1,0:T(8,128)S(1)}, f32[4,8,128]{2,1,0:T(8,128)S(1)}, u32[]{:S(2)}, u32[]{:S(2)}) collective-permute-start(f32[4,8,128]{2,1,0:T(8,128)S(1)} %get-tuple-element.55), channel_id=1, source_target_pairs={{0,32},{1,33},{2,34},{3,35},{4,36},{5,37},{6,38},{7,39},{8,40},{9,... | collective-permute-start | bytes 49160 | tf_op jit(solution)/shard_map/ppermute | solution.py:344
  27.2 5.2 %collective-permute-start.8 = (f32[4,8,128]{2,1,0:T(8,128)S(1)}, f32[4,8,128]{2,1,0:T(8,128)S(1)}, u32[]{:S(2)}, u32[]{:S(2)}) collective-permute-start(f32[4,8,128]{2,1,0:T(8,128)S(1)} %get-tuple-element.54), channel_id=1, source_target_pairs={{0,64},{1,65},{2,66},{3,67},{4,68},{5,69},{6,70},{7,71},{8,72},{9,... | collective-permute-start | bytes 49160 | tf_op jit(solution)/shard_map/ppermute | solution.py:344
  30.0 3.7 %collective-permute-start.9 = (f32[4,8,128]{2,1,0:T(8,128)S(1)}, f32[4,8,128]{2,1,0:T(8,128)S(1)}, u32[]{:S(2)}, u32[]{:S(2)}) collective-permute-start(f32[4,8,128]{2,1,0:T(8,128)S(1)} %get-tuple-element.53), channel_id=1, source_target_pairs={{0,96},{1,97},{2,98},{3,99},{4,100},{5,101},{6,102},{7,103},{8,104... | collective-permute-start | bytes 49160 | tf_op jit(solution)/shard_map/ppermute | solution.py:344

commit v4 on v3

--- a/solution.py
+++ b/solution.py
@@ -22,11 +22,9 @@
 CHUNKS = ROWS // CHUNK
 LOADS = 4
 LOAD = ROWS // LOADS
-FETCHES = 2
-FETCH = WBLK * CELLS // FETCHES
 TAIL = 64
 SECS = 4
-ROTATIONS = SECS - 1
+PARTNERS = SECS - 1
 GOALS = 80
 
 f32 = jnp.float32
@@ -94,8 +92,8 @@
         )
         sums = jnp.dot(counts, right, preferred_element_type=f32)
         for t, target in enumerate(targets):
-            for slot in range(ROTATIONS):
-                row = (t * ROTATIONS + slot) * BLK
+            for slot in range(PARTNERS):
+                row = (t * PARTNERS + slot) * BLK
                 for j in range(2):
                     target[slot * COUPLED + first + j] = sums[
                         row : row + BLK, j * CELLS : (j + 1) * CELLS
@@ -111,9 +109,9 @@
     device = lax.shift_right_logical(goal, BLK.bit_length() - 1)
     to_col = jnp.bitwise_and(device, columns - 1)
     to_sec = lax.shift_right_logical(device, columns.bit_length() - 1)
-    slot = jnp.bitwise_and(to_sec - sec + (SECS - 1), SECS - 1)
+    slot = jnp.where(sec == SECS - 1, to_sec, jnp.full_like(to_sec, sec))
     place = jnp.where(to_col == col, 0, jnp.where(to_col == jnp.bitwise_xor(col, 1), 1, 2))
-    row = (place * ROTATIONS + slot) * BLK + jnp.bitwise_and(goal, BLK - 1)
+    row = (place * PARTNERS + slot) * BLK + jnp.bitwise_and(goal, BLK - 1)
     position = lax.broadcasted_iota(jnp.int32, (1, entries), 1)
     row = jnp.where(position < used, row, -1)
     combination = weight * BLK + jnp.bitwise_and(source, BLK - 1)
@@ -128,25 +126,15 @@
     return jnp.concatenate([counts, counts], axis=1)
 
 
-def first_kernel(
-    state, mask, listing, weights, count, own, near, far, stacked, counts, sea,
-    tail, mask_buf, list_buf, w_buf, surface, products, sems, w_sems,
-):
-    small = [
+def setup_kernel(state, mask, listing, count, left, counts, sea, tail, mask_buf, list_buf, surface, sems):
+    copies = [
         pltpu.make_async_copy(listing, list_buf, sems.at[0]),
-        pltpu.make_async_copy(state.at[pl.ds(ROWS - TAIL, TAIL)], tail, sems.at[1]),
-        pltpu.make_async_copy(mask, mask_buf, sems.at[2]),
+        pltpu.make_async_copy(mask, mask_buf, sems.at[1]),
+        pltpu.make_async_copy(state.at[pl.ds(ROWS - TAIL, TAIL)], tail, sems.at[2]),
     ]
-    for copy in small:
+    for copy in copies:
         copy.start()
-
-    def fetch(i):
-        rows = pl.ds(i * FETCH, FETCH)
-        return pltpu.make_async_copy(weights.at[rows], w_buf.at[rows], w_sems.at[i])
-
-    for i in range(FETCHES):
-        fetch(i).start()
-    for copy in small:
+    for copy in copies:
         copy.wait()
     counts[...] = count_entries(list_buf[...], count[0, 0])
     cells = mask_buf[...].astype(f32)
@@ -159,18 +147,19 @@
             )
 
     per_component(component)
-    left = doubled(surface[...])
+    left[...] = doubled(surface[...])
+
+
+def first_kernel(left, counts, weights, own, near, far, stacked, products):
     for p in range(PAIRS):
         base = p * 2 * CELLS
-        if base % FETCH == 0:
-            fetch(base // FETCH).wait()
-        high0, low0 = split(w_buf[base : base + CELLS])
-        high1, low1 = split(w_buf[base + CELLS : base + 2 * CELLS])
+        high0, low0 = split(weights[base : base + CELLS])
+        high1, low1 = split(weights[base + CELLS : base + 2 * CELLS])
         both = jnp.concatenate(
             [jnp.concatenate([high0, high1], axis=1), jnp.concatenate([low0, low1], axis=1)], axis=0
         )
         stacked[base : base + 2 * CELLS] = both
-        multiply(left, both, products, p)
+        multiply(left[...], both, products, p)
     deliver(counts[...], products, (own, near, far))
 
 
@@ -327,8 +316,17 @@
 
     near = table(lambda s, c: (s, c ^ 1))
     far = table(lambda s, c: (s, c + 1 if c % 2 else c - 1))
-    turns = [table(lambda s, c, k=k: (s + k, c)) for k in range(1, secs)]
-    return near, far, turns
+    def swap(a):
+        def move(s, c):
+            if s == a:
+                return secs - 1, c
+            if s == secs - 1:
+                return a, c
+            return s, c ^ 1
+
+        return table(move)
+
+    return near, far, [swap(a) for a in range(PARTNERS)]
 
 
 def along_col(own, near, far, tables):
@@ -342,7 +340,7 @@
     total = own + from_near + from_far
     got = [
         lax.ppermute(total[k * COUPLED : (k + 1) * COUPLED], AXES, tables[2][k])
-        for k in range(ROTATIONS)
+        for k in range(PARTNERS)
     ]
     return total, got
 
@@ -354,7 +352,7 @@
     listing = jnp.transpose(pairings, (2, 0, 1))
     points = ROWS * CELLS
     full = ((ROWS, CELLS), f32)
-    payload = ((ROTATIONS * COUPLED, BLK, CELLS), f32)
+    payload = ((PARTNERS * COUPLED, BLK, CELLS), f32)
     face = ((COUPLED, BLK, CELLS), f32)
     stack = ((PAIRS * 2 * CELLS, 2 * CELLS), bf16)
     table = ((GOALS, 2 * WBLK * BLK), bf16)
@@ -362,25 +360,32 @@
     products = pltpu.VMEM((COUPLED, WBLK * BLK, CELLS), f32)
     wide = pltpu.VMEM((TAIL, CELLS), f32)
 
-    own, near, far, stacked, counts, sea = call(
-        first_kernel,
-        [payload, payload, payload, stack, table, ((BLK, CELLS), f32)],
-        [state, surface_mask[0], listing, remap_weights[0], pairing_count],
-        4,
+    left, counts, sea = call(
+        setup_kernel,
+        [((2 * WIDE, 2 * CELLS), bf16), table, ((BLK, CELLS), f32)],
+        [state, surface_mask[0], listing, pairing_count],
+        3,
         [
             pltpu.VMEM((TAIL, CELLS), f32),
             pltpu.VMEM((BLK, CELLS), jnp.int32),
             pltpu.VMEM(listing.shape, jnp.int32),
-            pltpu.VMEM((WBLK * CELLS, CELLS), f32),
             surface,
-            products,
             pltpu.SemaphoreType.DMA((3,)),
-            pltpu.SemaphoreType.DMA((FETCHES,)),
         ],
-        6,
+        2,
+        1 << 24,
+        1 << 17,
+        in_smem=1,
+    )
+    own, near, far, stacked = call(
+        first_kernel,
+        [payload, payload, payload, stack],
+        [left, counts, remap_weights[0]],
+        0,
+        [products],
+        4,
         1 << 28,
         1 << 21,
-        in_smem=1,
     )
 
     parts = along_col(own, near, far, tables)

time: 35.5 us -> 31.2 us (0.88); the launches traced: 35.4 us -> 30.6 us
  starting transfers between devices: 19.8 us -> 17 us
  waiting for transfers between devices: 6.42 us -> 4.65 us
    ppermute x6, starting transfers between devices: 9.54 us -> 6.2 us  [along_sec(): lax.ppermute(total[k * COUPLED:(k + 1) * COUPLED], AXES, tables[2][k])]
    ppermute x6, waiting for transfers between devices: 3.64 us -> 2.43 us  [along_sec(): lax.ppermute(total[k * COUPLED:(k + 1) * COUPLED], AXES, tables[2][k])]
    ppermute x2, starting transfers between devices: 10.1 us -> 10.7 us  [along_col(): from_far = lax.ppermute(far, AXES, tables[1])]
    ppermute x2, waiting for transfers between devices: 2.77 us -> 2.21 us  [along_col(): from_far = lax.ppermute(far, AXES, tables[1])]
    pallas_call x5 -> x6, Pallas kernels: 8.42 us -> 8.1 us  [call(): pl.pallas_call(kernel, out_shape=[jax.ShapeDtypeStruct(shape, kind) for s...]
  transfers between devices with their start and end apart: 10 -> 10, of which waited for: 5 -> 3; matrix products, arithmetic and copies ran while one was open for 0% -> 0% of each run, Pallas kernels for 13% -> 15%
where the time goes in v4:
time: 31.2 us; the launch traced here: 30.6 us
  starting transfers between devices  17 us (54%)
  Pallas kernels  8.1 us (26%)
  waiting for transfers between devices  4.65 us (15%)
  between operations  0.84 us (3%)
    ppermute x2, starting transfers between devices, along_col(): from_far = lax.ppermute(far, AXES, tables[1])  10.7 us
    pallas_call x6, Pallas kernels, call(): pl.pallas_call(kernel, out_shape=[jax.ShapeDtypeStruct(shape, kind) for s...  8.1 us
    ppermute x6, starting transfers between devices, along_sec(): lax.ppermute(total[k * COUPLED:(k + 1) * COUPLED], AXES, tables[2][k])  6.2 us
    ppermute x6, waiting for transfers between devices, along_sec(): lax.ppermute(total[k * COUPLED:(k + 1) * COUPLED], AXES, tables[2][k])  2.43 us
    ppermute x2, waiting for transfers between devices, along_col(): from_far = lax.ppermute(far, AXES, tables[1])  2.21 us
  transfers between devices with their start and end apart: 10, of which 3 were waited for; matrix products, arithmetic and copies ran while one was open for 0% of the time, Pallas kernels for 15%

profile of v4, /device:TPU:0, one launch (start us, length us, event | category | flops | bytes accessed | tf_op | source)
XLA Modules:
  0.0 30.6 jit_solution(16393771997179231673)
XLA Ops:
  0.0 0.0 copy-start
  0.7 1.0 %shard_map.64 = (bf16[64,256]{1,0:T(8,128)(2,1)S(1)}, bf16[80,256]{1,0:T(8,128)(2,1)S(1)}, f32[8,128]{1,0:T(8,128)S(1)}) custom-call(f32[5120,128]{1,0:T(8,128)} %bitcast.7, s32[8,128]{1,0:T(8,128)} %bitcast.10, s32[3,1,54]{2,1,0:T(1,128)} %bitcast.11, s32[1,1]{1,0:T(1,128)S(6)} %copy.7.count), custom_call_target="tpu_custom_call" | custom-call | flops 16777216 | bytes 131072 | tf_op jit(solution)/shard_map/pallas_call | solution.py:44
  1.7 0.0 copy-done
  1.8 0.5 %shard_map.65 = (f32[12,8,128]{2,1,0:T(8,128)S(1)}, f32[12,8,128]{2,1,0:T(8,128)S(1)}, f32[12,8,128]{2,1,0:T(8,128)S(1)}, bf16[2048,256]{1,0:T(8,128)(2,1)S(1)}) custom-call(bf16[64,256]{1,0:T(8,128)(2,1)S(1)} %get-tuple-element.30.left, bf16[80,256]{1,0:T(8,128)(2,1)S(1)} %get-tuple-element.31.counts, f32[2048,128]{1,0:T(8,128)S(1)} %bitcast.6), custom_call_target="tpu_custom_call" | custom-call | flops 268435456 | bytes 2097152 | tf_op jit(solution)/shard_map/pallas_call | solution.py:44
  2.3 5.8 %collective-permute-start.1 = (f32[12,8,128]{2,1,0:T(8,128)S(1)}, f32[12,8,128]{2,1,0:T(8,128)S(1)}, u32[]{:S(2)}, u32[]{:S(2)}) collective-permute-start(f32[12,8,128]{2,1,0:T(8,128)S(1)} %get-tuple-element.34), channel_id=1, source_target_pairs={{0,31},{1,2},{2,1},{3,4},{4,3},{5,6},{6,5},{7,8},{8,7},{9,10},{10,... | collective-permute-start | bytes 147464 | tf_op jit(solution)/shard_map/ppermute | solution.py:334
  8.1 0.0 collective-permute-start
  8.1 1.8 %collective-permute-done.1 = f32[12,8,128]{2,1,0:T(8,128)S(1)} collective-permute-done((f32[12,8,128]{2,1,0:T(8,128)S(1)}, f32[12,8,128]{2,1,0:T(8,128)S(1)}, u32[]{:S(2)}, u32[]{:S(2)}) %collective-permute-start.1) | collective-permute-done | bytes 49184 | tf_op jit(solution)/shard_map/ppermute | solution.py:334
  9.9 0.0 collective-permute-done
  9.9 3.1 %collective-permute-start.2 = (f32[4,8,128]{2,1,0:T(8,128)S(1)}, f32[4,8,128]{2,1,0:T(8,128)S(1)}, u32[]{:S(2)}, u32[]{:S(2)}) collective-permute-start(f32[4,8,128]{2,1,0:T(8,128)S(1)} %get-tuple-element.60), channel_id=1, source_target_pairs={{0,96},{1,97},{2,98},{3,99},{4,100},{5,101},{6,102},{7,103},{8,104... | collective-permute-start | bytes 49160 | tf_op jit(solution)/shard_map/ppermute | solution.py:342
  13.0 0.0 collective-permute-start.3
  13.0 0.5 %collective-permute-start.4 = (f32[4,8,128]{2,1,0:T(8,128)S(1)}, f32[4,8,128]{2,1,0:T(8,128)S(1)}, u32[]{:S(2)}, u32[]{:S(2)}) collective-permute-start(f32[4,8,128]{2,1,0:T(8,128)S(1)} %get-tuple-element.58), channel_id=1, source_target_pairs={{0,1},{1,0},{2,3},{3,2},{4,5},{5,4},{6,7},{7,6},{8,9},{9,8},{10,11... | collective-permute-start | bytes 49160 | tf_op jit(solution)/shard_map/ppermute | solution.py:342
  13.5 2.9 %shard_map.66 = (f32[5120,128]{1,0:T(8,128)S(1)}, f32[5120,128]{1,0:T(8,128)S(1)}, f32[5120,128]{1,0:T(8,128)S(1)}, f32[5120,128]{1,0:T(8,128)S(1)}, f32[4,8,128]{2,1,0:T(8,128)S(1)}, /*index=5*/f32[4,8,128]{2,1,0:T(8,128)S(1)}) custom-call(f32[5120,128]{1,0:T(8,128)} %bitcast.8, f32[5120,128]{1,0:T(8,128)} %bitcast.9, f32[8,128]{1,0:T(8,128)S(1)} %get-tuple-element.36.sea), custom_call_target="tpu_custom_call" | custom-call | flops 13107200 | bytes 15728640 | tf_op jit(solution)/shard_map/pallas_call | solution.py:44
  16.4 0.0 collective-permute-done.2.got1
  16.4 0.0 collective-permute-done.3.got2
  16.4 0.0 collective-permute-done.4.got3
  16.4 0.5 %shard_map.67 = (f32[4,8,128]{2,1,0:T(8,128)S(1)}, f32[12,8,128]{2,1,0:T(8,128)S(1)}, f32[12,8,128]{2,1,0:T(8,128)S(1)}, f32[12,8,128]{2,1,0:T(8,128)S(1)}) custom-call(f32[4,8,128]{2,1,0:T(8,128)S(1)} %collective-permute-done.2.got1, f32[4,8,128]{2,1,0:T(8,128)S(1)} %collective-permute-done.3.got2, f32[4,8,128]{2,1,0:T(8,128)S(1)} %collective-permute-done.4.got3, ...), custom_call_target="tpu_custom_call" | custom-call | flops 268435456 | bytes 2097152 | tf_op jit(solution)/shard_map/pallas_call | solution.py:44
  16.9 0.1 collective-permute-start.5
  17.0 4.9 %collective-permute-start.6 = (f32[12,8,128]{2,1,0:T(8,128)S(1)}, f32[12,8,128]{2,1,0:T(8,128)S(1)}, u32[]{:S(2)}, u32[]{:S(2)}) collective-permute-start(f32[12,8,128]{2,1,0:T(8,128)S(1)} %get-tuple-element.42), channel_id=1, source_target_pairs={{0,31},{1,2},{2,1},{3,4},{4,3},{5,6},{6,5},{7,8},{8,7},{9,10},{10,... | collective-permute-start | bytes 147464 | tf_op jit(solution)/shard_map/ppermute | solution.py:334
  21.8 1.6 %shard_map.68 = (f32[5120,128]{1,0:T(8,128)S(1)}, f32[5120,128]{1,0:T(8,128)S(1)}) custom-call(f32[4,8,128]{2,1,0:T(8,128)S(1)} %get-tuple-element.43.boundary, f32[5120,128]{1,0:T(8,128)S(1)} %get-tuple-element.44.c, f32[5120,128]{1,0:T(8,128)S(1)} %get-tuple-element.45.w, f32[5120,128]{1,0:T(8,128)S(1)} %get-tuple-element.46.e, ...), custom_call_target="tpu_custom_call" | custom-call | flops 5898240 | bytes 31457280 | tf_op jit(solution)/shard_map/pallas_call | solution.py:44
  23.4 0.0 collective-permute-done.5
  23.5 0.4 %collective-permute-done.6 = f32[12,8,128]{2,1,0:T(8,128)S(1)} collective-permute-done((f32[12,8,128]{2,1,0:T(8,128)S(1)}, f32[12,8,128]{2,1,0:T(8,128)S(1)}, u32[]{:S(2)}, u32[]{:S(2)}) %collective-permute-start.6) | collective-permute-done | bytes 49184 | tf_op jit(solution)/shard_map/ppermute | solution.py:334
  23.9 2.1 %collective-permute-start.7 = (f32[4,8,128]{2,1,0:T(8,128)S(1)}, f32[4,8,128]{2,1,0:T(8,128)S(1)}, u32[]{:S(2)}, u32[]{:S(2)}) collective-permute-start(f32[4,8,128]{2,1,0:T(8,128)S(1)} %get-tuple-element.57), channel_id=1, source_target_pairs={{0,96},{1,97},{2,98},{3,99},{4,100},{5,101},{6,102},{7,103},{8,104... | collective-permute-start | bytes 49160 | tf_op jit(solution)/shard_map/ppermute | solution.py:342
  26.0 0.0 collective-permute-start.8
  26.0 0.5 %collective-permute-start.9 = (f32[4,8,128]{2,1,0:T(8,128)S(1)}, f32[4,8,128]{2,1,0:T(8,128)S(1)}, u32[]{:S(2)}, u32[]{:S(2)}) collective-permute-start(f32[4,8,128]{2,1,0:T(8,128)S(1)} %get-tuple-element.55), channel_id=1, source_target_pairs={{0,1},{1,0},{2,3},{3,2},{4,5},{5,4},{6,7},{7,6},{8,9},{9,8},{10,11... | collective-permute-start | bytes 49160 | tf_op jit(solution)/shard_map/ppermute | solution.py:342
  26.5 2.4 %collective-permute-done.7.got1 = f32[4,8,128]{2,1,0:T(8,128)S(1)} collective-permute-done((f32[4,8,128]{2,1,0:T(8,128)S(1)}, f32[4,8,128]{2,1,0:T(8,128)S(1)}, u32[]{:S(2)}, u32[]{:S(2)}) %collective-permute-start.7) | collective-permute-done | bytes 16416 | tf_op jit(solution)/shard_map/ppermute | solution.py:342
  29.0 0.0 collective-permute-done.8.got2
  29.0 0.0 collective-permute-done.9.got3
  29.0 1.7 %shard_map.69 = f32[5120,128]{1,0:T(8,128)} custom-call(f32[4,8,128]{2,1,0:T(8,128)S(1)} %collective-permute-done.7.got1, f32[4,8,128]{2,1,0:T(8,128)S(1)} %collective-permute-done.8.got2, f32[4,8,128]{2,1,0:T(8,128)S(1)} %collective-permute-done.9.got3, f32[5120,128]{1,0:T(8,128)S(1)} %get-tuple-element.53.u, f32[5120,128]{1,0:T(8,128)S(1)} %get-tuple-element.54.g), custom_call_target="tpu_custom_call" | custom-call | flops 1310720 | bytes 7864320 | tf_op jit(solution)/shard_map/pallas_call | solution.py:44
  (4 shorter events, 0.0 us)
Async XLA Ops:
  0.0 1.7 %copy-start = (f32[1,2048,128]{2,1,0:T(8,128)S(1)}, f32[1,2048,128]{2,1,0:T(8,128)}, u32[]{:S(2)}) copy-start(f32[1,2048,128]{2,1,0:T(8,128)} %param.11) | copy-start | bytes 3145732
  2.3 7.6 %collective-permute-start.1 = (f32[12,8,128]{2,1,0:T(8,128)S(1)}, f32[12,8,128]{2,1,0:T(8,128)S(1)}, u32[]{:S(2)}, u32[]{:S(2)}) collective-permute-start(f32[12,8,128]{2,1,0:T(8,128)S(1)} %get-tuple-element.34), channel_id=1, source_target_pairs={{0,31},{1,2},{2,1},{3,4},{4,3},{5,6},{6,5},{7,8},{8,7},{9,10},{10,... | collective-permute-start | bytes 147464 | tf_op jit(solution)/shard_map/ppermute | solution.py:334
  8.1 1.8 %collective-permute-start = (f32[12,8,128]{2,1,0:T(8,128)S(1)}, f32[12,8,128]{2,1,0:T(8,128)S(1)}, u32[]{:S(2)}, u32[]{:S(2)}) collective-permute-start(f32[12,8,128]{2,1,0:T(8,128)S(1)} %get-tuple-element.33), channel_id=1, source_target_pairs={{0,1},{1,0},{2,3},{3,2},{4,5},{5,4},{6,7},{7,6},{8,9},{9,8},{10,11... | collective-permute-start | bytes 147464 | tf_op jit(solution)/shard_map/ppermute | solution.py:333
  9.9 6.5 %collective-permute-start.2 = (f32[4,8,128]{2,1,0:T(8,128)S(1)}, f32[4,8,128]{2,1,0:T(8,128)S(1)}, u32[]{:S(2)}, u32[]{:S(2)}) collective-permute-start(f32[4,8,128]{2,1,0:T(8,128)S(1)} %get-tuple-element.60), channel_id=1, source_target_pairs={{0,96},{1,97},{2,98},{3,99},{4,100},{5,101},{6,102},{7,103},{8,104... | collective-permute-start | bytes 49160 | tf_op jit(solution)/shard_map/ppermute | solution.py:342
  13.0 3.4 %collective-permute-start.3 = (f32[4,8,128]{2,1,0:T(8,128)S(1)}, f32[4,8,128]{2,1,0:T(8,128)S(1)}, u32[]{:S(2)}, u32[]{:S(2)}) collective-permute-start(f32[4,8,128]{2,1,0:T(8,128)S(1)} %get-tuple-element.59), channel_id=1, source_target_pairs={{0,1},{1,0},{2,3},{3,2},{4,5},{5,4},{6,7},{7,6},{8,9},{9,8},{10,11... | collective-permute-start | bytes 49160 | tf_op jit(solution)/shard_map/ppermute | solution.py:342
  13.0 3.4 %collective-permute-start.4 = (f32[4,8,128]{2,1,0:T(8,128)S(1)}, f32[4,8,128]{2,1,0:T(8,128)S(1)}, u32[]{:S(2)}, u32[]{:S(2)}) collective-permute-start(f32[4,8,128]{2,1,0:T(8,128)S(1)} %get-tuple-element.58), channel_id=1, source_target_pairs={{0,1},{1,0},{2,3},{3,2},{4,5},{5,4},{6,7},{7,6},{8,9},{9,8},{10,11... | collective-permute-start | bytes 49160 | tf_op jit(solution)/shard_map/ppermute | solution.py:342
  16.9 6.6 %collective-permute-start.5 = (f32[12,8,128]{2,1,0:T(8,128)S(1)}, f32[12,8,128]{2,1,0:T(8,128)S(1)}, u32[]{:S(2)}, u32[]{:S(2)}) collective-permute-start(f32[12,8,128]{2,1,0:T(8,128)S(1)} %get-tuple-element.41), channel_id=1, source_target_pairs={{0,1},{1,0},{2,3},{3,2},{4,5},{5,4},{6,7},{7,6},{8,9},{9,8},{10,11... | collective-permute-start | bytes 147464 | tf_op jit(solution)/shard_map/ppermute | solution.py:333
  17.0 6.9 %collective-permute-start.6 = (f32[12,8,128]{2,1,0:T(8,128)S(1)}, f32[12,8,128]{2,1,0:T(8,128)S(1)}, u32[]{:S(2)}, u32[]{:S(2)}) collective-permute-start(f32[12,8,128]{2,1,0:T(8,128)S(1)} %get-tuple-element.42), channel_id=1, source_target_pairs={{0,31},{1,2},{2,1},{3,4},{4,3},{5,6},{6,5},{7,8},{8,7},{9,10},{10,... | collective-permute-start | bytes 147464 | tf_op jit(solution)/shard_map/ppermute | solution.py:334
  23.9 5.0 %collective-permute-start.7 = (f32[4,8,128]{2,1,0:T(8,128)S(1)}, f32[4,8,128]{2,1,0:T(8,128)S(1)}, u32[]{:S(2)}, u32[]{:S(2)}) collective-permute-start(f32[4,8,128]{2,1,0:T(8,128)S(1)} %get-tuple-element.57), channel_id=1, source_target_pairs={{0,96},{1,97},{2,98},{3,99},{4,100},{5,101},{6,102},{7,103},{8,104... | collective-permute-start | bytes 49160 | tf_op jit(solution)/shard_map/ppermute | solution.py:342
  26.0 2.9 %collective-permute-start.8 = (f32[4,8,128]{2,1,0:T(8,128)S(1)}, f32[4,8,128]{2,1,0:T(8,128)S(1)}, u32[]{:S(2)}, u32[]{:S(2)}) collective-permute-start(f32[4,8,128]{2,1,0:T(8,128)S(1)} %get-tuple-element.56), channel_id=1, source_target_pairs={{0,1},{1,0},{2,3},{3,2},{4,5},{5,4},{6,7},{7,6},{8,9},{9,8},{10,11... | collective-permute-start | bytes 49160 | tf_op jit(solution)/shard_map/ppermute | solution.py:342
  26.0 2.9 %collective-permute-start.9 = (f32[4,8,128]{2,1,0:T(8,128)S(1)}, f32[4,8,128]{2,1,0:T(8,128)S(1)}, u32[]{:S(2)}, u32[]{:S(2)}) collective-permute-start(f32[4,8,128]{2,1,0:T(8,128)S(1)} %get-tuple-element.55), channel_id=1, source_target_pairs={{0,1},{1,0},{2,3},{3,2},{4,5},{5,4},{6,7},{7,6},{8,9},{9,8},{10,11... | collective-permute-start | bytes 49160 | tf_op jit(solution)/shard_map/ppermute | solution.py:342
